TPU v7x, 256 devices: a whole 4x4x8 slice. The times are simulated.
256 devices in a mesh: pairs: 32 (over z, y_hi, core), aux: 8 (over x, y_lo).
Axes of the slice: x: 4, y: 4 (y_hi: 2, y_lo: 2; y = y_hi * 2 + y_lo), z: 8, core: 2. Of those that a mesh axis runs over, the one named last changes fastest.
Arguments:
- amplitudes: float32 [64, 256, 256], P('pairs'), may hold values from -6 to 6
- factors: float32 [384, 256, 256], P('aux', 'pairs'), may hold values from -0.078125 to 0.078125
- occ_factors: float32 [384, 8, 8], P('aux'), may hold values from -0.5 to 0.5
Outputs:
- resid: float32 [64, 256, 256], P(None, 'pairs', 'aux')
All inputs are finite; a program needn't handle non-finite values.
Results may differ from a plain program's by a relative error of at most 0.0001.
Values sent between devices are 32-bit elements; how exact they have to be, the bound alone decides.
A program may use at most 64 MiB of HBM per device.

v0:
```python
import jax
import jax.numpy as jnp
from jax import lax
from jax.sharding import PartitionSpec as P

highest = lax.Precision.HIGHEST


def both_sides(running, amps, row_block):
    mixed_terms = jnp.einsum("icd,pbd->picb", amps, row_block, precision=highest)
    return running + jnp.einsum("pac,picb->iab", row_block, mixed_terms, precision=highest)


def shards(amplitudes, factors, occ_factors):
    local_pairs = amplitudes.shape[0]
    virt_width = amplitudes.shape[1]
    aux_local = factors.shape[0]
    occupied = occ_factors.shape[1]
    total_pairs = occupied * occupied
    aux_rank = lax.axis_index("aux")
    column_count = virt_width // lax.axis_size("aux")
    col_start = aux_rank * column_count
    amp_cols = lax.dynamic_slice_in_dim(amplitudes, col_start, column_count, 2)
    amp_flip = jnp.swapaxes(lax.dynamic_slice_in_dim(amplitudes, col_start, column_count, 1), 1, 2)

    def whole_step(running, block_index):
        row_block = lax.dynamic_slice_in_dim(factors, block_index * 2, 2, 0)
        whole_rows = lax.all_gather(row_block, "pairs", axis=1, tiled=True)
        return (both_sides(running, amplitudes, whole_rows), None)

    particle, unused = lax.scan(
        whole_step,
        jnp.zeros((local_pairs, virt_width, virt_width), jnp.float32),
        jnp.arange(aux_local // 2),
    )
    coupling = jnp.einsum("pik,pjl->ijkl", occ_factors, occ_factors, precision=highest).reshape(
        total_pairs, total_pairs
    )
    particle, coupling = lax.psum((particle, coupling), "aux")
    part_cols = lax.dynamic_slice_in_dim(particle, col_start, column_count, 2)
    part_flip = jnp.swapaxes(lax.dynamic_slice_in_dim(particle, col_start, column_count, 1), 1, 2)
    part_cols, part_flip, amp_cols, amp_flip = (
        lax.all_to_all(part_cols, "pairs", split_axis=1, concat_axis=0, tiled=True),
        lax.all_to_all(part_flip, "pairs", split_axis=1, concat_axis=0, tiled=True),
        lax.all_to_all(amp_cols, "pairs", split_axis=1, concat_axis=0, tiled=True),
        lax.all_to_all(amp_flip, "pairs", split_axis=1, concat_axis=0, tiled=True),
    )
    straight = part_cols + jnp.einsum("pk,kab->pab", coupling, amp_cols, precision=highest)
    turned = part_flip + jnp.einsum("pk,kab->pab", coupling, amp_flip, precision=highest)
    rows_here = turned.shape[1]
    turned = (
        turned.reshape(occupied, occupied, rows_here, column_count)
        .transpose(1, 0, 2, 3)
        .reshape(total_pairs, rows_here, column_count)
    )
    return straight + turned


def solution(mesh):
    placed = (P("pairs", None, None), P("aux", "pairs", None), P("aux", None, None))
    return jax.shard_map(
        shards, mesh=mesh, in_specs=placed, out_specs=P(None, "pairs", "aux"), check_vma=False
    )
```

profile of v0, /device:TPU:1, one launch (start us, length us, event | category | flops | bytes accessed | tf_op | source)
XLA Modules:
  0.0 1193.5 jit_solution(1170505517774073015)
XLA Ops:
  6.5 1064.0 %while.11 = (s32[]{:T(128)}, f32[2,256,256]{1,2,0:T(8,128)S(1)}, s32[24]{0:T(128)S(1)}, f32[48,8,256]{2,1,0:T(8,128)}, f32[2,256,256]{2,1,0:T(8,128)}, /*index=5*/s32[]{:T(128)}, s32[1]{0:T(128)}, s32[]{:T(128)}, s32[]{:T(128)}) while((s32[]{:T(128)}, f32[2,256,256]{1,2,0:T(8,128)S(1)}, s32[24]{0:T(128)S(1)}, ...), condition=%wide.region_1.2_spmd.clone, body=%wide.region_0.1_spmd.clone.sunk | while | flops 1610874880 | bytes 7389385 | solution.py:31
  8.6 47.7 %all_gather.5 = f32[2,256,256]{2,1,0:T(8,128)S(1)} all-gather(f32[2,8,256]{2,1,0:T(8,128)S(1)} %constant_dynamic-slice_fusion.5), channel_id=1, replica_groups=mesh['pairs'=32,'aux'=8] {'pairs'}, dimensions={1}, use_global_device_ids=true | all-gather | bytes 540672 | tf_op jit(solution)/shard_map/while/body/eval_jaxpr/all_gather | solution.py:28
  57.4 1.3 fusion.23
  60.8 38.1 %all_gather.5 = f32[2,256,256]{2,1,0:T(8,128)S(1)} all-gather(f32[2,8,256]{2,1,0:T(8,128)S(1)} %constant_dynamic-slice_fusion.5), channel_id=1, replica_groups=mesh['pairs'=32,'aux'=8] {'pairs'}, dimensions={1}, use_global_device_ids=true | all-gather | bytes 540672 | tf_op jit(solution)/shard_map/while/body/eval_jaxpr/all_gather | solution.py:28
  100.0 1.3 fusion.23
  103.3 41.1 %all_gather.5 = f32[2,256,256]{2,1,0:T(8,128)S(1)} all-gather(f32[2,8,256]{2,1,0:T(8,128)S(1)} %constant_dynamic-slice_fusion.5), channel_id=1, replica_groups=mesh['pairs'=32,'aux'=8] {'pairs'}, dimensions={1}, use_global_device_ids=true | all-gather | bytes 540672 | tf_op jit(solution)/shard_map/while/body/eval_jaxpr/all_gather | solution.py:28
  145.5 1.3 fusion.23
  148.9 38.1 %all_gather.5 = f32[2,256,256]{2,1,0:T(8,128)S(1)} all-gather(f32[2,8,256]{2,1,0:T(8,128)S(1)} %constant_dynamic-slice_fusion.5), channel_id=1, replica_groups=mesh['pairs'=32,'aux'=8] {'pairs'}, dimensions={1}, use_global_device_ids=true | all-gather | bytes 540672 | tf_op jit(solution)/shard_map/while/body/eval_jaxpr/all_gather | solution.py:28
  187.0 1.0 convolution_bitcast_fusion.4
  188.1 1.3 fusion.23
  191.5 41.1 %all_gather.5 = f32[2,256,256]{2,1,0:T(8,128)S(1)} all-gather(f32[2,8,256]{2,1,0:T(8,128)S(1)} %constant_dynamic-slice_fusion.5), channel_id=1, replica_groups=mesh['pairs'=32,'aux'=8] {'pairs'}, dimensions={1}, use_global_device_ids=true | all-gather | bytes 540672 | tf_op jit(solution)/shard_map/while/body/eval_jaxpr/all_gather | solution.py:28
  233.6 1.3 fusion.23
  237.0 38.1 %all_gather.5 = f32[2,256,256]{2,1,0:T(8,128)S(1)} all-gather(f32[2,8,256]{2,1,0:T(8,128)S(1)} %constant_dynamic-slice_fusion.5), channel_id=1, replica_groups=mesh['pairs'=32,'aux'=8] {'pairs'}, dimensions={1}, use_global_device_ids=true | all-gather | bytes 540672 | tf_op jit(solution)/shard_map/while/body/eval_jaxpr/all_gather | solution.py:28
  276.2 1.3 fusion.23
  279.6 41.1 %all_gather.5 = f32[2,256,256]{2,1,0:T(8,128)S(1)} all-gather(f32[2,8,256]{2,1,0:T(8,128)S(1)} %constant_dynamic-slice_fusion.5), channel_id=1, replica_groups=mesh['pairs'=32,'aux'=8] {'pairs'}, dimensions={1}, use_global_device_ids=true | all-gather | bytes 540672 | tf_op jit(solution)/shard_map/while/body/eval_jaxpr/all_gather | solution.py:28
  321.7 1.3 fusion.23
  325.1 38.1 %all_gather.5 = f32[2,256,256]{2,1,0:T(8,128)S(1)} all-gather(f32[2,8,256]{2,1,0:T(8,128)S(1)} %constant_dynamic-slice_fusion.5), channel_id=1, replica_groups=mesh['pairs'=32,'aux'=8] {'pairs'}, dimensions={1}, use_global_device_ids=true | all-gather | bytes 540672 | tf_op jit(solution)/shard_map/while/body/eval_jaxpr/all_gather | solution.py:28
  363.3 1.0 convolution_bitcast_fusion.4
  364.3 1.3 fusion.23
  367.7 41.1 %all_gather.5 = f32[2,256,256]{2,1,0:T(8,128)S(1)} all-gather(f32[2,8,256]{2,1,0:T(8,128)S(1)} %constant_dynamic-slice_fusion.5), channel_id=1, replica_groups=mesh['pairs'=32,'aux'=8] {'pairs'}, dimensions={1}, use_global_device_ids=true | all-gather | bytes 540672 | tf_op jit(solution)/shard_map/while/body/eval_jaxpr/all_gather | solution.py:28
  409.9 1.3 fusion.23
  413.3 38.1 %all_gather.5 = f32[2,256,256]{2,1,0:T(8,128)S(1)} all-gather(f32[2,8,256]{2,1,0:T(8,128)S(1)} %constant_dynamic-slice_fusion.5), channel_id=1, replica_groups=mesh['pairs'=32,'aux'=8] {'pairs'}, dimensions={1}, use_global_device_ids=true | all-gather | bytes 540672 | tf_op jit(solution)/shard_map/while/body/eval_jaxpr/all_gather | solution.py:28
  451.4 1.0 convolution_bitcast_fusion.4
  452.4 1.3 fusion.23
  455.8 41.1 %all_gather.5 = f32[2,256,256]{2,1,0:T(8,128)S(1)} all-gather(f32[2,8,256]{2,1,0:T(8,128)S(1)} %constant_dynamic-slice_fusion.5), channel_id=1, replica_groups=mesh['pairs'=32,'aux'=8] {'pairs'}, dimensions={1}, use_global_device_ids=true | all-gather | bytes 540672 | tf_op jit(solution)/shard_map/while/body/eval_jaxpr/all_gather | solution.py:28
  498.0 1.3 fusion.23
  501.4 38.1 %all_gather.5 = f32[2,256,256]{2,1,0:T(8,128)S(1)} all-gather(f32[2,8,256]{2,1,0:T(8,128)S(1)} %constant_dynamic-slice_fusion.5), channel_id=1, replica_groups=mesh['pairs'=32,'aux'=8] {'pairs'}, dimensions={1}, use_global_device_ids=true | all-gather | bytes 540672 | tf_op jit(solution)/shard_map/while/body/eval_jaxpr/all_gather | solution.py:28
  540.5 1.3 fusion.23
  543.9 41.1 %all_gather.5 = f32[2,256,256]{2,1,0:T(8,128)S(1)} all-gather(f32[2,8,256]{2,1,0:T(8,128)S(1)} %constant_dynamic-slice_fusion.5), channel_id=1, replica_groups=mesh['pairs'=32,'aux'=8] {'pairs'}, dimensions={1}, use_global_device_ids=true | all-gather | bytes 540672 | tf_op jit(solution)/shard_map/while/body/eval_jaxpr/all_gather | solution.py:28
  586.1 1.3 fusion.23
  589.5 38.1 %all_gather.5 = f32[2,256,256]{2,1,0:T(8,128)S(1)} all-gather(f32[2,8,256]{2,1,0:T(8,128)S(1)} %constant_dynamic-slice_fusion.5), channel_id=1, replica_groups=mesh['pairs'=32,'aux'=8] {'pairs'}, dimensions={1}, use_global_device_ids=true | all-gather | bytes 540672 | tf_op jit(solution)/shard_map/while/body/eval_jaxpr/all_gather | solution.py:28
  628.7 1.3 fusion.23
  632.1 41.1 %all_gather.5 = f32[2,256,256]{2,1,0:T(8,128)S(1)} all-gather(f32[2,8,256]{2,1,0:T(8,128)S(1)} %constant_dynamic-slice_fusion.5), channel_id=1, replica_groups=mesh['pairs'=32,'aux'=8] {'pairs'}, dimensions={1}, use_global_device_ids=true | all-gather | bytes 540672 | tf_op jit(solution)/shard_map/while/body/eval_jaxpr/all_gather | solution.py:28
  674.2 1.3 fusion.23
  677.6 38.1 %all_gather.5 = f32[2,256,256]{2,1,0:T(8,128)S(1)} all-gather(f32[2,8,256]{2,1,0:T(8,128)S(1)} %constant_dynamic-slice_fusion.5), channel_id=1, replica_groups=mesh['pairs'=32,'aux'=8] {'pairs'}, dimensions={1}, use_global_device_ids=true | all-gather | bytes 540672 | tf_op jit(solution)/shard_map/while/body/eval_jaxpr/all_gather | solution.py:28
  715.7 1.0 convolution_bitcast_fusion.4
  716.8 1.3 fusion.23
  720.2 41.1 %all_gather.5 = f32[2,256,256]{2,1,0:T(8,128)S(1)} all-gather(f32[2,8,256]{2,1,0:T(8,128)S(1)} %constant_dynamic-slice_fusion.5), channel_id=1, replica_groups=mesh['pairs'=32,'aux'=8] {'pairs'}, dimensions={1}, use_global_device_ids=true | all-gather | bytes 540672 | tf_op jit(solution)/shard_map/while/body/eval_jaxpr/all_gather | solution.py:28
  762.3 1.3 fusion.23
  765.7 38.1 %all_gather.5 = f32[2,256,256]{2,1,0:T(8,128)S(1)} all-gather(f32[2,8,256]{2,1,0:T(8,128)S(1)} %constant_dynamic-slice_fusion.5), channel_id=1, replica_groups=mesh['pairs'=32,'aux'=8] {'pairs'}, dimensions={1}, use_global_device_ids=true | all-gather | bytes 540672 | tf_op jit(solution)/shard_map/while/body/eval_jaxpr/all_gather | solution.py:28
  803.8 1.0 convolution_bitcast_fusion.4
  804.9 1.3 fusion.23
  808.3 41.1 %all_gather.5 = f32[2,256,256]{2,1,0:T(8,128)S(1)} all-gather(f32[2,8,256]{2,1,0:T(8,128)S(1)} %constant_dynamic-slice_fusion.5), channel_id=1, replica_groups=mesh['pairs'=32,'aux'=8] {'pairs'}, dimensions={1}, use_global_device_ids=true | all-gather | bytes 540672 | tf_op jit(solution)/shard_map/while/body/eval_jaxpr/all_gather | solution.py:28
  850.5 1.3 fusion.23
  853.8 38.1 %all_gather.5 = f32[2,256,256]{2,1,0:T(8,128)S(1)} all-gather(f32[2,8,256]{2,1,0:T(8,128)S(1)} %constant_dynamic-slice_fusion.5), channel_id=1, replica_groups=mesh['pairs'=32,'aux'=8] {'pairs'}, dimensions={1}, use_global_device_ids=true | all-gather | bytes 540672 | tf_op jit(solution)/shard_map/while/body/eval_jaxpr/all_gather | solution.py:28
  893.0 1.3 fusion.23
  896.4 41.1 %all_gather.5 = f32[2,256,256]{2,1,0:T(8,128)S(1)} all-gather(f32[2,8,256]{2,1,0:T(8,128)S(1)} %constant_dynamic-slice_fusion.5), channel_id=1, replica_groups=mesh['pairs'=32,'aux'=8] {'pairs'}, dimensions={1}, use_global_device_ids=true | all-gather | bytes 540672 | tf_op jit(solution)/shard_map/while/body/eval_jaxpr/all_gather | solution.py:28
  938.6 1.3 fusion.23
  942.0 38.1 %all_gather.5 = f32[2,256,256]{2,1,0:T(8,128)S(1)} all-gather(f32[2,8,256]{2,1,0:T(8,128)S(1)} %constant_dynamic-slice_fusion.5), channel_id=1, replica_groups=mesh['pairs'=32,'aux'=8] {'pairs'}, dimensions={1}, use_global_device_ids=true | all-gather | bytes 540672 | tf_op jit(solution)/shard_map/while/body/eval_jaxpr/all_gather | solution.py:28
  981.1 1.3 fusion.23
  984.5 41.1 %all_gather.5 = f32[2,256,256]{2,1,0:T(8,128)S(1)} all-gather(f32[2,8,256]{2,1,0:T(8,128)S(1)} %constant_dynamic-slice_fusion.5), channel_id=1, replica_groups=mesh['pairs'=32,'aux'=8] {'pairs'}, dimensions={1}, use_global_device_ids=true | all-gather | bytes 540672 | tf_op jit(solution)/shard_map/while/body/eval_jaxpr/all_gather | solution.py:28
  1026.7 1.3 fusion.23
  1030.1 38.1 %all_gather.5 = f32[2,256,256]{2,1,0:T(8,128)S(1)} all-gather(f32[2,8,256]{2,1,0:T(8,128)S(1)} %constant_dynamic-slice_fusion.5), channel_id=1, replica_groups=mesh['pairs'=32,'aux'=8] {'pairs'}, dimensions={1}, use_global_device_ids=true | all-gather | bytes 540672 | tf_op jit(solution)/shard_map/while/body/eval_jaxpr/all_gather | solution.py:28
  1068.2 1.0 convolution_bitcast_fusion.4
  1069.3 1.3 fusion.23
  1073.7 6.1 all-to-all-start.3
  1082.0 7.6 all-to-all-done.3
  1089.6 3.9 all-to-all-start.1
  1093.5 26.1 %psum.15 = f32[64,64]{1,0:T(8,128)S(1)} all-reduce(f32[64,64]{1,0:T(8,128)S(1)} %reshape.11), channel_id=1, replica_groups=mesh['pairs'=32,'aux'=8] {'aux'}, use_global_device_ids=true, to_apply=%region_3.4 | all-reduce | flops 4096 | bytes 32768 | tf_op jit(solution)/shard_map/psum | solution.py:39
  1121.2 22.7 %all-reduce.2.cloned.1.call-done = f32[2,256,256]{2,0,1:T(2,128)} async-done(((f32[2,256,256]{2,0,1:T(2,128)}), f32[2,256,256]{2,0,1:T(2,128)}) %all-reduce.2.cloned.1.call-update) | async-done | bytes 524304 | tf_op jit(solution)/shard_map/psum | solution.py:39
  1145.9 15.2 %all-to-all-start.2 = ((f32[32,1,512]{2,1,0:T(1,128)}), f32[32,1,512]{2,1,0:T(1,128)S(1)}, u32[]{:S(2)}, u32[]{:S(2)}) async-start(f32[32,1,512]{2,1,0:T(1,128)} %reshape.22), calls=%async_computation.2 | async-start | bytes 131072 | tf_op jit(solution)/shard_map/all_to_all | solution.py:44
  1164.6 6.3 all-to-all-done.2
  1170.9 3.9 all-to-all-start
  1176.6 8.2 all-to-all-done
  (168 shorter events, 67.9 us)
Async XLA Ops:
  6.5 1073.3 %copy-start = (f32[48,8,8]{0,2,1:T(8,128)S(1)}, f32[48,8,8]{0,2,1:T(8,128)}, u32[]{:S(2)}) copy-start(f32[48,8,8]{0,2,1:T(8,128)} %param.7) | copy-start | bytes 36868
  6.5 1137.5 %all-reduce.2.cloned.1.call-start = ((), (), s32[]{:S(2)}) async-start(), calls=%async_computation.4 | async-start | bytes 1048576 | tf_op jit(solution)/shard_map/psum | solution.py:39
  6.5 49.8 %copy-start.1 = (f32[2,256,256]{2,1,0:T(8,128)S(1)}, f32[2,256,256]{2,1,0:T(8,128)}, u32[]{:S(2)}) copy-start(f32[2,256,256]{2,1,0:T(8,128)} %get-tuple-element.114) | copy-start | bytes 1572868 | tf_op jit(solution)/shard_map/while
  58.7 40.2 %copy-start.1 = (f32[2,256,256]{2,1,0:T(8,128)S(1)}, f32[2,256,256]{2,1,0:T(8,128)}, u32[]{:S(2)}) copy-start(f32[2,256,256]{2,1,0:T(8,128)} %get-tuple-element.114) | copy-start | bytes 1572868 | tf_op jit(solution)/shard_map/while
  101.2 43.2 %copy-start.1 = (f32[2,256,256]{2,1,0:T(8,128)S(1)}, f32[2,256,256]{2,1,0:T(8,128)}, u32[]{:S(2)}) copy-start(f32[2,256,256]{2,1,0:T(8,128)} %get-tuple-element.114) | copy-start | bytes 1572868 | tf_op jit(solution)/shard_map/while
  146.8 40.2 %copy-start.1 = (f32[2,256,256]{2,1,0:T(8,128)S(1)}, f32[2,256,256]{2,1,0:T(8,128)}, u32[]{:S(2)}) copy-start(f32[2,256,256]{2,1,0:T(8,128)} %get-tuple-element.114) | copy-start | bytes 1572868 | tf_op jit(solution)/shard_map/while
  189.4 43.2 %copy-start.1 = (f32[2,256,256]{2,1,0:T(8,128)S(1)}, f32[2,256,256]{2,1,0:T(8,128)}, u32[]{:S(2)}) copy-start(f32[2,256,256]{2,1,0:T(8,128)} %get-tuple-element.114) | copy-start | bytes 1572868 | tf_op jit(solution)/shard_map/while
  234.9 40.2 %copy-start.1 = (f32[2,256,256]{2,1,0:T(8,128)S(1)}, f32[2,256,256]{2,1,0:T(8,128)}, u32[]{:S(2)}) copy-start(f32[2,256,256]{2,1,0:T(8,128)} %get-tuple-element.114) | copy-start | bytes 1572868 | tf_op jit(solution)/shard_map/while
  277.5 43.2 %copy-start.1 = (f32[2,256,256]{2,1,0:T(8,128)S(1)}, f32[2,256,256]{2,1,0:T(8,128)}, u32[]{:S(2)}) copy-start(f32[2,256,256]{2,1,0:T(8,128)} %get-tuple-element.114) | copy-start | bytes 1572868 | tf_op jit(solution)/shard_map/while
  323.0 40.2 %copy-start.1 = (f32[2,256,256]{2,1,0:T(8,128)S(1)}, f32[2,256,256]{2,1,0:T(8,128)}, u32[]{:S(2)}) copy-start(f32[2,256,256]{2,1,0:T(8,128)} %get-tuple-element.114) | copy-start | bytes 1572868 | tf_op jit(solution)/shard_map/while
  365.6 43.2 %copy-start.1 = (f32[2,256,256]{2,1,0:T(8,128)S(1)}, f32[2,256,256]{2,1,0:T(8,128)}, u32[]{:S(2)}) copy-start(f32[2,256,256]{2,1,0:T(8,128)} %get-tuple-element.114) | copy-start | bytes 1572868 | tf_op jit(solution)/shard_map/while
  411.1 40.2 %copy-start.1 = (f32[2,256,256]{2,1,0:T(8,128)S(1)}, f32[2,256,256]{2,1,0:T(8,128)}, u32[]{:S(2)}) copy-start(f32[2,256,256]{2,1,0:T(8,128)} %get-tuple-element.114) | copy-start | bytes 1572868 | tf_op jit(solution)/shard_map/while
  453.7 43.2 %copy-start.1 = (f32[2,256,256]{2,1,0:T(8,128)S(1)}, f32[2,256,256]{2,1,0:T(8,128)}, u32[]{:S(2)}) copy-start(f32[2,256,256]{2,1,0:T(8,128)} %get-tuple-element.114) | copy-start | bytes 1572868 | tf_op jit(solution)/shard_map/while
  499.3 40.2 %copy-start.1 = (f32[2,256,256]{2,1,0:T(8,128)S(1)}, f32[2,256,256]{2,1,0:T(8,128)}, u32[]{:S(2)}) copy-start(f32[2,256,256]{2,1,0:T(8,128)} %get-tuple-element.114) | copy-start | bytes 1572868 | tf_op jit(solution)/shard_map/while
  541.8 43.2 %copy-start.1 = (f32[2,256,256]{2,1,0:T(8,128)S(1)}, f32[2,256,256]{2,1,0:T(8,128)}, u32[]{:S(2)}) copy-start(f32[2,256,256]{2,1,0:T(8,128)} %get-tuple-element.114) | copy-start | bytes 1572868 | tf_op jit(solution)/shard_map/while
  587.4 40.2 %copy-start.1 = (f32[2,256,256]{2,1,0:T(8,128)S(1)}, f32[2,256,256]{2,1,0:T(8,128)}, u32[]{:S(2)}) copy-start(f32[2,256,256]{2,1,0:T(8,128)} %get-tuple-element.114) | copy-start | bytes 1572868 | tf_op jit(solution)/shard_map/while
  629.9 43.2 %copy-start.1 = (f32[2,256,256]{2,1,0:T(8,128)S(1)}, f32[2,256,256]{2,1,0:T(8,128)}, u32[]{:S(2)}) copy-start(f32[2,256,256]{2,1,0:T(8,128)} %get-tuple-element.114) | copy-start | bytes 1572868 | tf_op jit(solution)/shard_map/while
  675.5 40.2 %copy-start.1 = (f32[2,256,256]{2,1,0:T(8,128)S(1)}, f32[2,256,256]{2,1,0:T(8,128)}, u32[]{:S(2)}) copy-start(f32[2,256,256]{2,1,0:T(8,128)} %get-tuple-element.114) | copy-start | bytes 1572868 | tf_op jit(solution)/shard_map/while
  718.1 43.2 %copy-start.1 = (f32[2,256,256]{2,1,0:T(8,128)S(1)}, f32[2,256,256]{2,1,0:T(8,128)}, u32[]{:S(2)}) copy-start(f32[2,256,256]{2,1,0:T(8,128)} %get-tuple-element.114) | copy-start | bytes 1572868 | tf_op jit(solution)/shard_map/while
  763.6 40.2 %copy-start.1 = (f32[2,256,256]{2,1,0:T(8,128)S(1)}, f32[2,256,256]{2,1,0:T(8,128)}, u32[]{:S(2)}) copy-start(f32[2,256,256]{2,1,0:T(8,128)} %get-tuple-element.114) | copy-start | bytes 1572868 | tf_op jit(solution)/shard_map/while
  806.2 43.2 %copy-start.1 = (f32[2,256,256]{2,1,0:T(8,128)S(1)}, f32[2,256,256]{2,1,0:T(8,128)}, u32[]{:S(2)}) copy-start(f32[2,256,256]{2,1,0:T(8,128)} %get-tuple-element.114) | copy-start | bytes 1572868 | tf_op jit(solution)/shard_map/while
  851.7 40.2 %copy-start.1 = (f32[2,256,256]{2,1,0:T(8,128)S(1)}, f32[2,256,256]{2,1,0:T(8,128)}, u32[]{:S(2)}) copy-start(f32[2,256,256]{2,1,0:T(8,128)} %get-tuple-element.114) | copy-start | bytes 1572868 | tf_op jit(solution)/shard_map/while
  894.3 43.2 %copy-start.1 = (f32[2,256,256]{2,1,0:T(8,128)S(1)}, f32[2,256,256]{2,1,0:T(8,128)}, u32[]{:S(2)}) copy-start(f32[2,256,256]{2,1,0:T(8,128)} %get-tuple-element.114) | copy-start | bytes 1572868 | tf_op jit(solution)/shard_map/while
  939.9 40.2 %copy-start.1 = (f32[2,256,256]{2,1,0:T(8,128)S(1)}, f32[2,256,256]{2,1,0:T(8,128)}, u32[]{:S(2)}) copy-start(f32[2,256,256]{2,1,0:T(8,128)} %get-tuple-element.114) | copy-start | bytes 1572868 | tf_op jit(solution)/shard_map/while
  982.4 43.2 %copy-start.1 = (f32[2,256,256]{2,1,0:T(8,128)S(1)}, f32[2,256,256]{2,1,0:T(8,128)}, u32[]{:S(2)}) copy-start(f32[2,256,256]{2,1,0:T(8,128)} %get-tuple-element.114) | copy-start | bytes 1572868 | tf_op jit(solution)/shard_map/while
  1028.0 40.2 %copy-start.1 = (f32[2,256,256]{2,1,0:T(8,128)S(1)}, f32[2,256,256]{2,1,0:T(8,128)}, u32[]{:S(2)}) copy-start(f32[2,256,256]{2,1,0:T(8,128)} %get-tuple-element.114) | copy-start | bytes 1572868 | tf_op jit(solution)/shard_map/while
  1071.5 1.0 copy-start.2
  1073.7 15.9 %all-to-all-start.3 = ((f32[32,1,512]{2,1,0:T(1,128)}), f32[32,1,512]{2,1,0:T(1,128)S(1)}, u32[]{:S(2)}, u32[]{:S(2)}) async-start(f32[32,1,512]{2,1,0:T(1,128)} %reshape.24), calls=%async_computation.3 | async-start | bytes 131072 | tf_op jit(solution)/shard_map/all_to_all | solution.py:46
  1089.6 56.3 %all-to-all-start.1 = ((f32[32,1,512]{2,1,0:T(1,128)}), f32[32,1,512]{2,1,0:T(1,128)S(1)}, u32[]{:S(2)}, u32[]{:S(2)}) async-start(f32[32,1,512]{2,1,0:T(1,128)} %reshape.28), calls=%async_computation.1 | async-start | bytes 131072 | tf_op jit(solution)/shard_map/all_to_all | solution.py:45
  1145.9 25.0 %all-to-all-start.2 = ((f32[32,1,512]{2,1,0:T(1,128)}), f32[32,1,512]{2,1,0:T(1,128)S(1)}, u32[]{:S(2)}, u32[]{:S(2)}) async-start(f32[32,1,512]{2,1,0:T(1,128)} %reshape.22), calls=%async_computation.2 | async-start | bytes 131072 | tf_op jit(solution)/shard_map/all_to_all | solution.py:44
  1162.4 1.0 copy-start.3
  1170.9 13.8 %all-to-all-start = ((f32[32,1,512]{2,1,0:T(1,128)}), f32[32,1,512]{2,1,0:T(1,128)S(1)}, u32[]{:S(2)}, u32[]{:S(2)}) async-start(f32[32,1,512]{2,1,0:T(1,128)} %reshape.26), calls=%async_computation | async-start | bytes 131072 | tf_op jit(solution)/shard_map/all_to_all | solution.py:43
Sparse Core Ops, SparseCore 0:
  1071.7 72.2 all-reduce.1
where the time goes:
time: 1200 us; the launch traced here: 1190 us
  blocking collectives  984 us (82%)
  matrix products  56.4 us (5%)
  waiting for transfers between devices  44.8 us (4%)
  local copies, waits for them, and re-layouts  44.5 us (4%)
  starting transfers between devices  29.1 us (2%)
  loops' own time  17.9 us (1%)
  between operations  13.7 us (1%)
    all_gather x24, blocking collectives, whole_step(): whole_rows = lax.all_gather(row_block, 'pairs', axis=1, tiled=True)  957 us
    dot_general x24, matrix products, both_sides(): jnp.einsum('pac,picb->iab', row_block, mixed_terms, precision=highest)  30.3 us
    psum x1, blocking collectives, shards(): particle, coupling = lax.psum((particle, coupling), 'aux')  26.1 us
    dot_general x24, matrix products, both_sides(): jnp.einsum('icd,pbd->picb', amps, row_block, precision=highest)  24.8 us
  transfers between devices with their start and end apart: 5, of which 4 were waited for; matrix products, arithmetic and copies ran while one was open for 1% of the time, Pallas kernels for 0%

commit v1 on v0

v1 whole, which is shorter than its diff:
```python
import functools

import jax
import jax.numpy as jnp
from jax import lax
from jax.experimental import pallas as pl
from jax.experimental.pallas import tpu as pltpu
from jax.sharding import PartitionSpec as P

highest = lax.Precision.HIGHEST
F32 = jnp.float32
BF16 = jnp.bfloat16

Z = 8
K = 4
W = 8
PLANE = K * W
OFFSETS = 5
CHUNKS = 4


def remote(src, dst, send_sem, recv_sem, p, w):
    return pltpu.make_async_remote_copy(
        src_ref=src,
        dst_ref=dst,
        send_sem=send_sem,
        recv_sem=recv_sem,
        device_id={"pairs": p, "aux": w},
        device_id_type=pl.DeviceIdType.MESH,
    )


def wait_bytes(ref, sem):
    pltpu.make_async_copy(ref, ref, sem).wait()


def place():
    p = lax.axis_index("pairs")
    w = lax.axis_index("aux")
    return p, w, p // K, lax.rem(p, K)


def greet(p, w, z):
    barrier = pltpu.get_barrier_semaphore()
    k = lax.rem(p, K)
    m = w * K + k

    def plane_peer(t, c):
        n = lax.rem(m + t, PLANE)
        pl.semaphore_signal(
            barrier, inc=1, device_id={"pairs": z * K + lax.rem(n, K), "aux": n // K},
            device_id_type=pl.DeviceIdType.MESH)
        return c

    def column_peer(t, c):
        pl.semaphore_signal(
            barrier, inc=1, device_id={"pairs": lax.rem(p + t, Z * K), "aux": w},
            device_id_type=pl.DeviceIdType.MESH)
        return c

    lax.fori_loop(1, PLANE, plane_peer, 0)
    lax.fori_loop(1, Z * K, column_peer, 0)
    pl.semaphore_wait(barrier, PLANE + Z * K - 2)


def gather_kernel(amp, fac, ball, sall, flip, slots, mine,
                  ex_send, ex_recv, a_send, a_recv, s_send, s_recv, ring_send, ring_recv):
    p, w, z, k = place()
    m = w * K + k
    greet(p, w, z)
    per = ball.shape[0] // CHUNKS
    up = lax.rem(z + 1, Z) * K + k
    down = lax.rem(z + Z - 1, Z) * K + k

    def exchange(g, t):
        kk = lax.rem(k + t, K)
        src = fac.at[pl.ds(kk * (per * CHUNKS) + g * per, per)]
        dst = ball.at[pl.ds(g * per, per), pl.ds(pl.multiple_of(8 * p, 8), 8), :]
        if t == 0:
            return pltpu.make_async_copy(src, dst, ex_recv.at[g])
        return remote(src, dst, ex_send.at[g], ex_recv.at[g], z * K + kk, w)

    for g in range(CHUNKS):
        for t in range(K):
            exchange(g, t).start()

    def straight(t):
        kk = lax.rem(k + t, K)
        src = amp.at[:, pl.ds(pl.multiple_of((w * K + kk) * 8, 8), 8), :]
        dst = slots.at[pl.ds(2 * k, 2)]
        if t == 0:
            return pltpu.make_async_copy(src, dst, a_recv)
        return remote(src, dst, a_send, a_recv, z * K + kk, w)

    def turned(s, kk):
        src = flip.at[s, pl.ds(pl.multiple_of((w * K + kk) * 8, 8), 8), :]
        dst = slots.at[Z + z]
        near = pltpu.make_async_copy(src, dst, a_recv)
        far = remote(src, dst, a_send, a_recv, (2 * k + s) * K + kk, w)
        return near, far, jnp.logical_and(2 * k + s == z, kk == k)

    for t in range(K):
        straight(t).start()
    for s in range(2):
        flip[s] = amp[s].T
    for s in range(2):
        for kk in range(K):
            near, far, here = turned(s, kk)
            pl.when(here)(near.start)
            pl.when(jnp.logical_not(here))(far.start)

    def hops(way, g):
        return 4 if (way + g) % 2 == 0 else 3

    def ring(way, g, h):
        origin = lax.rem(z + (Z - h if way == 0 else h), Z)
        part = ball.at[pl.ds(g * per, per), pl.ds(pl.multiple_of(origin * 32, 32), 32), :]
        return remote(part, part, ring_send.at[way, g, h], ring_recv.at[way, g, h], up if way == 0 else down, w)

    def arrived(way, g, h):
        origin = lax.rem(z + (Z - 1 - h if way == 0 else 1 + h), Z)
        part = ball.at[pl.ds(g * per, per), pl.ds(pl.multiple_of(origin * 32, 32), 32), :]
        return remote(part, part, ring_send.at[way, g, h], ring_recv.at[way, g, h], up if way == 0 else down, w)

    for g in range(CHUNKS):
        wait_bytes(ball.at[pl.ds(g * per, per), pl.ds(pl.multiple_of(z * 32, 32), 32), :], ex_recv.at[g])
        for way in range(2):
            ring(way, g, 0).start()

    wait_bytes(slots, a_recv)
    for d in range(OFFSETS):
        j = lax.rem(z + d, Z)
        mine[d] = slots[j] + slots[Z + j]

    def share(t):
        n = lax.rem(m + t, PLANE)
        return remote(mine, sall.at[:, pl.ds(pl.multiple_of(m * 8, 8), 8), :], s_send, s_recv,
                      z * K + lax.rem(n, K), n // K)

    pltpu.make_async_copy(mine, sall.at[:, pl.ds(pl.multiple_of(m * 8, 8), 8), :], s_recv).start()

    def share_start(t, c):
        share(t).start()
        return c

    lax.fori_loop(1, PLANE, share_start, 0)

    for h in range(1, 4):
        for g in range(CHUNKS):
            for way in range(2):
                if h < hops(way, g):
                    arrived(way, g, h - 1).wait_recv()
                    ring(way, g, h).start()
    for g in range(CHUNKS):
        for way in range(2):
            arrived(way, g, hops(way, g) - 1).wait_recv()
    wait_bytes(sall, s_recv)
    for g in range(CHUNKS):
        for t in range(1, K):
            exchange(g, t).wait_send()
        for way in range(2):
            for h in range(hops(way, g)):
                ring(way, g, h).wait_send()
    for t in range(1, K):
        straight(t).wait_send()
    for s in range(2):
        for kk in range(K):
            near, far, here = turned(s, kk)
            pl.when(jnp.logical_not(here))(far.wait_send)
    wait_bytes(sall.at[:, pl.ds(0, 8 * (PLANE - 1)), :], s_send)


def gather(amplitudes, factors):
    aux_local, rows, virt = factors.shape
    local = aux_local // K
    vm = pl.BlockSpec(memory_space=pltpu.VMEM)
    dma = pltpu.SemaphoreType.DMA
    return pl.pallas_call(
        gather_kernel,
        out_shape=(
            jax.ShapeDtypeStruct((local, virt, virt), F32),
            jax.ShapeDtypeStruct((OFFSETS, virt, virt), F32),
        ),
        in_specs=[vm, vm],
        out_specs=(vm, vm),
        scratch_shapes=[
            pltpu.VMEM((2, virt, virt), F32),
            pltpu.VMEM((2 * Z, 8, virt), F32),
            pltpu.VMEM((OFFSETS, 8, virt), F32),
            dma((CHUNKS,)), dma((CHUNKS,)),
            dma(()), dma(()), dma(()), dma(()),
            dma((2, CHUNKS, 4)), dma((2, CHUNKS, 4)),
        ],
        compiler_params=pltpu.CompilerParams(
            collective_id=0, has_side_effects=True, vmem_limit_bytes=40 << 20),
        name="gather",
    )(amplitudes, factors)


def split(x):
    hi = x.astype(BF16)
    return hi, (x - hi.astype(F32)).astype(BF16)


def dot(a, b):
    return lax.dot_general(a, b, (((1,), (0,)), ((), ())), preferred_element_type=F32)


def dot_t(a, b):
    return lax.dot_general(a, b, (((1,), (1,)), ((), ())), preferred_element_type=F32)


def ladder_kernel(ball, sall, out, s_hi, s_lo, y_hi, y_lo, acc):
    per = y_hi.shape[0]
    virt = ball.shape[1]
    for d in range(OFFSETS):
        s_hi[d], s_lo[d] = split(sall[d])

    def chunk(g, c):
        b_hi, b_lo = split(ball[pl.ds(g * per, per)].reshape(per * virt, virt))
        for d in range(OFFSETS):
            y = dot(b_hi, s_hi[d]) + dot(b_hi, s_lo[d]) + dot(b_lo, s_hi[d])
            hi, lo = split(y)
            for q in range(per):
                y_hi[q, d * virt:(d + 1) * virt] = hi[q * virt:(q + 1) * virt]
                y_lo[q, d * virt:(d + 1) * virt] = lo[q * virt:(q + 1) * virt]
        total = None
        for q in range(per):
            bh, bl = b_hi[q * virt:(q + 1) * virt], b_lo[q * virt:(q + 1) * virt]
            term = dot_t(y_hi[q], bh) + dot_t(y_hi[q], bl) + dot_t(y_lo[q], bh)
            total = term if total is None else total + term
        acc[...] += total
        return c

    acc[...] = jnp.zeros_like(acc)
    lax.fori_loop(0, ball.shape[0] // per, chunk, 0)
    for d in range(OFFSETS):
        r = acc[d * virt:(d + 1) * virt]
        if d < 4:
            out[d] = r
        else:
            out[7] = r
        if 1 <= d <= 3:
            out[3 + d] = r.T


def ladder(ball, sall):
    virt = ball.shape[1]
    per = 3
    vm = pl.BlockSpec(memory_space=pltpu.VMEM)
    return pl.pallas_call(
        ladder_kernel,
        out_shape=jax.ShapeDtypeStruct((Z, virt, virt), F32),
        in_specs=[vm, vm],
        out_specs=vm,
        scratch_shapes=[
            pltpu.VMEM((OFFSETS, virt, virt), BF16),
            pltpu.VMEM((OFFSETS, virt, virt), BF16),
            pltpu.VMEM((per, OFFSETS * virt, virt), BF16),
            pltpu.VMEM((per, OFFSETS * virt, virt), BF16),
            pltpu.VMEM((OFFSETS * virt, virt), F32),
        ],
        compiler_params=pltpu.CompilerParams(vmem_limit_bytes=48 << 20),
        name="ladder",
    )(ball, sall)


def where_to():
    order = []
    for z in range(Z):
        for m in range(8):
            if m < 4:
                i, j = (z + m) % 8, z
            elif m < 7:
                i, j = z, (z + m - 3) % 8
            else:
                i, j = (z + 4) % 8, z
            order.append(i * 8 + j)
    return order


def scatter_kernel(part, hole, out, sib, half, slots, turn, last,
                   c_send, c_recv, r_send, r_recv, f_send, f_recv):
    p, w, z, k = place()
    greet(p, w, z)
    core = lax.rem(k, 2)
    up_half = k // 2
    other = p + 1 - 2 * core
    virt = part.shape[1]
    rows = virt // W

    def swap(v):
        return remote(part.at[pl.ds(4 * v + 2 * (1 - core), 2)], sib.at[pl.ds(2 * v, 2)],
                      c_send.at[v], c_recv.at[v], other, w)

    for v in range(2):
        swap(v).start()
    for v in range(2):
        swap(v).wait_recv()
        half[2 * v:2 * v + 2] = part[pl.ds(4 * v + 2 * core, 2)] + sib[2 * v:2 * v + 2]

    me = up_half * W + w

    def spread(t):
        n = lax.rem(me + t, 2 * W)
        v, ww = n // W, lax.rem(n, W)
        src = half.at[pl.ds(2 * v, 2), pl.ds(pl.multiple_of(ww * rows, rows), rows), :]
        return src, v, ww

    def spread_start(t, c):
        src, v, ww = spread(t)
        remote(src, slots.at[me], r_send, r_recv, z * K + v * 2 + core, ww).start()
        return c

    own, _, _ = spread(0)
    pltpu.make_async_copy(own, slots.at[me], r_recv).start()
    lax.fori_loop(1, 2 * W, spread_start, 0)
    wait_bytes(slots, r_recv)
    for s in range(2):
        total = slots[0, s]
        for n in range(1, 2 * W):
            total = total + slots[n, s]
        turn[s] = total.T

    def final(t):
        q = lax.rem(p + t, Z * K)
        return turn.at[:, pl.ds(pl.multiple_of(q * 8, 8), 8), :], q

    def final_start(t, c):
        src, q = final(t)
        remote(src, last.at[pl.ds(2 * p, 2)], f_send, f_recv, q, w).start()
        return c

    mine, _ = final(0)
    pltpu.make_async_copy(mine, last.at[pl.ds(2 * p, 2)], f_recv).start()
    lax.fori_loop(1, Z * K, final_start, 0)
    wait_bytes(last, f_recv)
    for slot, pair in enumerate(where_to()):
        out[pair] = last[slot] + hole[pair]
    for v in range(2):
        swap(v).wait_send()
    wait_bytes(slots.at[pl.ds(0, 2 * W - 1)], r_send)
    wait_bytes(last.at[pl.ds(0, 2 * (Z * K - 1))], f_send)


def scatter(part, hole):
    virt = part.shape[1]
    rows = virt // W
    vm = pl.BlockSpec(memory_space=pltpu.VMEM)
    dma = pltpu.SemaphoreType.DMA
    return pl.pallas_call(
        scatter_kernel,
        out_shape=jax.ShapeDtypeStruct(hole.shape, F32),
        in_specs=[vm, vm],
        out_specs=vm,
        scratch_shapes=[
            pltpu.VMEM((4, virt, virt), F32),
            pltpu.VMEM((4, virt, virt), F32),
            pltpu.VMEM((2 * W, 2, rows, virt), F32),
            pltpu.VMEM((2, virt, rows), F32),
            pltpu.VMEM((2 * Z * K, 8, rows), F32),
            dma((2,)), dma((2,)), dma(()), dma(()), dma(()), dma(()),
        ],
        compiler_params=pltpu.CompilerParams(
            collective_id=1, has_side_effects=True, vmem_limit_bytes=40 << 20),
        name="scatter",
    )(part, hole)


def hole_ladder(amplitudes, occ_factors):
    virt = amplitudes.shape[1]
    occupied = occ_factors.shape[1]
    pairs = occupied * occupied
    columns = virt // lax.axis_size("aux")
    start = lax.axis_index("aux") * columns
    cols = lax.dynamic_slice_in_dim(amplitudes, start, columns, 2)
    flip = jnp.swapaxes(lax.dynamic_slice_in_dim(amplitudes, start, columns, 1), 1, 2)
    cols = lax.all_to_all(cols, "pairs", split_axis=1, concat_axis=0, tiled=True)
    flip = lax.all_to_all(flip, "pairs", split_axis=1, concat_axis=0, tiled=True)
    rows = cols.shape[1]
    flip = flip.reshape(occupied, occupied, rows, columns).transpose(1, 0, 2, 3).reshape(pairs, rows, columns)
    coupling = jnp.einsum("pik,pjl->ijkl", occ_factors, occ_factors, precision=highest).reshape(pairs, pairs)
    coupling = lax.psum(coupling, "aux")
    return jnp.einsum("pk,kab->pab", coupling, cols + flip, precision=highest)


def shards(amplitudes, factors, occ_factors):
    hole = hole_ladder(amplitudes, occ_factors)
    ball, sall = gather(amplitudes, factors)
    part = ladder(ball, sall)
    return scatter(part, hole)


def solution(mesh):
    placed = (P("pairs", None, None), P("aux", "pairs", None), P("aux", None, None))
    return jax.shard_map(
        shards, mesh=mesh, in_specs=placed, out_specs=P(None, "pairs", "aux"), check_vma=False
    )
```

time: 1200 us -> 166 us (0.14)
  blocking collectives: 984 us -> 26.4 us
  Pallas kernels: 0 us -> 102 us
  matrix products: 56.4 us -> 0.95 us
  waiting for transfers between devices: 44.8 us -> 7.89 us
  local copies, waits for them, and re-layouts: 44.5 us -> 8.25 us
  loops' own time: 17.9 us -> 0 us
  between operations: 13.7 us -> 0.22 us
    all_gather x24 -> x0, blocking collectives: 957 us -> none  [whole_step(): whole_rows = lax.all_gather(row_block, 'pairs', axis=1, tiled=True)]
    pallas_call x0 -> x3, Pallas kernels: none -> 102 us  [the longest x1 43.9 us: gather(): pl.pallas_call(gather_kernel, out_shape=(jax.ShapeDtypeStruct((local, vir...]
    dot_general x49 -> x1, matrix products: 55.8 us -> 0.67 us  [hole_ladder(): jnp.einsum('pik,pjl->ijkl', occ_factors, occ_factors, precision=highest)]
    dynamic_slice x50 -> x2, local copies, waits for them, and re-layouts: 33.5 us -> 2.02 us  [the longest x1 1.16 us: hole_ladder(): cols = lax.dynamic_slice_in_dim(amplitudes, start, columns, 2)]
    psum x1 -> x0, waiting for transfers between devices: 22.7 us -> none  [shards(): particle, coupling = lax.psum((particle, coupling), 'aux')]
    another operation x1 -> x0, loops' own time: 17.9 us -> none  [shards(): lax.scan(whole_step, jnp.zeros((local_pairs, virt_width, virt_width), jnp...]
    all_to_all x4 -> x2, waiting for transfers between devices: 22.1 us -> 7.89 us  [the longest x1 7.89 us: hole_ladder(): lax.all_to_all(cols, 'pairs', split_axis=1, concat_axis=0, tiled=True)]
    all_to_all x4 -> x2, starting transfers between devices: 29.1 us -> 17.3 us  [the longest x1 12.8 us: hole_ladder(): lax.all_to_all(cols, 'pairs', split_axis=1, concat_axis=0, tiled=True)]
  transfers between devices with their start and end apart: 5 -> 2, of which waited for: 4 -> 1; matrix products, arithmetic and copies ran while one was open for 1% -> 3% of each run, Pallas kernels for 0% -> 38%
where the time goes in v1:
time: 166 us
  Pallas kernels  102 us (61%)
  blocking collectives  26.4 us (16%)
  starting transfers between devices  17.3 us (10%)
  local copies, waits for them, and re-layouts  8.25 us (5%)
  waiting for transfers between devices  7.89 us (5%)
  other arithmetic  2.48 us (1%)
    pallas_call x1, Pallas kernels, gather(): pl.pallas_call(gather_kernel, out_shape=(jax.ShapeDtypeStruct((local, vir...  43.9 us
    pallas_call x1, Pallas kernels, scatter(): pl.pallas_call(scatter_kernel, out_shape=jax.ShapeDtypeStruct(hole.shape,...  40 us
    psum x1, blocking collectives, hole_ladder(): coupling = lax.psum(coupling, 'aux')  26.4 us
    pallas_call x1, Pallas kernels, ladder(): pl.pallas_call(ladder_kernel, out_shape=jax.ShapeDtypeStruct((Z, virt, vi...  18.3 us
    all_to_all x1, starting transfers between devices, hole_ladder(): lax.all_to_all(cols, 'pairs', split_axis=1, concat_axis=0, tiled=True)  12.8 us
    all_to_all x1, waiting for transfers between devices, hole_ladder(): lax.all_to_all(cols, 'pairs', split_axis=1, concat_axis=0, tiled=True)  7.89 us
    all_to_all x1, starting transfers between devices, hole_ladder(): lax.all_to_all(flip, 'pairs', split_axis=1, concat_axis=0, tiled=True)  4.51 us
    unnamed x15, local copies, waits for them, and re-layouts  4.32 us
  transfers between devices with their start and end apart: 2, of which 1 were waited for; matrix products, arithmetic and copies ran while one was open for 3% of the time, Pallas kernels for 38%

profile of v1, /device:TPU:1, one launch (start us, length us, event | category | flops | bytes accessed | tf_op | source)
XLA Modules:
  0.0 165.7 jit_solution(4866082976280675667)
XLA Ops:
  0.0 0.0 copy-start
  0.0 0.0 copy-start.2
  0.0 0.0 copy-start.3
  0.0 1.2 constant_dynamic-slice_fusion.1
  1.2 0.2 copy.31
  1.4 0.9 reshape.16
  2.3 12.8 %all-to-all-start = ((f32[32,1,512]{2,1,0:T(1,128)}), f32[32,1,512]{2,1,0:T(1,128)S(1)}, u32[]{:S(2)}, u32[]{:S(2)}) async-start(f32[32,1,512]{2,1,0:T(1,128)} %reshape.16), calls=%async_computation | async-start | bytes 131072 | tf_op jit(solution)/shard_map/all_to_all | solution.py:378
  15.1 0.9 constant_dynamic-slice_fusion
  15.9 0.1 copy.27
  16.1 0.9 reshape.18
  17.0 7.9 %all-to-all-done = f32[32,1,512]{2,1,0:T(1,128)S(1)} async-done(((f32[32,1,512]{2,1,0:T(1,128)}), f32[32,1,512]{2,1,0:T(1,128)S(1)}, u32[]{:S(2)}, u32[]{:S(2)}) %all-to-all-start) | async-done | bytes 65568 | tf_op jit(solution)/shard_map/all_to_all | solution.py:378
  24.9 4.5 %all-to-all-start.1 = ((f32[32,1,512]{2,1,0:T(1,128)}), f32[32,1,512]{2,1,0:T(1,128)}, u32[]{:S(2)}, u32[]{:S(2)}) async-start(f32[32,1,512]{2,1,0:T(1,128)} %reshape.18), calls=%async_computation.1 | async-start | bytes 131072 | tf_op jit(solution)/shard_map/all_to_all | solution.py:379
  29.4 0.0 copy-done
  29.4 0.7 convolution_bitcast_fusion
  30.1 0.0 copy-done.2
  30.1 0.0 copy-done.3
  30.1 43.9 %gather.1 = (f32[12,256,256]{2,1,0:T(8,128)S(1)}, f32[5,256,256]{2,1,0:T(8,128)S(1)}) custom-call(f32[2,256,256]{2,1,0:T(8,128)S(1)} %copy-done.2, f32[48,8,256]{2,1,0:T(8,128)S(1)} %copy-done.3), custom_call_target="tpu_custom_call" | custom-call | tf_op jit(solution)/shard_map/gather/pallas_call | solution.py:178
  74.0 0.0 copy-start.1
  74.0 1.7 copy-done.1
  75.7 0.1 copy.15
  75.8 0.1 reshape.10
  75.9 18.3 %ladder.1.part = f32[8,256,256]{2,1,0:T(8,128)S(1)} custom-call(f32[12,256,256]{2,1,0:T(8,128)} %copy-done.1, f32[5,256,256]{2,1,0:T(8,128)S(1)} %get-tuple-element.8.sall), custom_call_target="tpu_custom_call" | custom-call | tf_op jit(solution)/shard_map/ladder/pallas_call | solution.py:251
  94.2 26.4 %psum.7 = f32[64,64]{1,0:T(8,128)S(1)} all-reduce(f32[64,64]{1,0:T(8,128)S(1)} %reshape.10), channel_id=1, replica_groups=mesh['pairs'=32,'aux'=8] {'aux'}, use_global_device_ids=true, to_apply=%region_0.0 | all-reduce | flops 4096 | bytes 32768 | tf_op jit(solution)/shard_map/psum | solution.py:383
  120.6 0.5 broadcast
  121.1 0.8 reduce
  122.0 0.2 reshape.17
  122.2 0.0 all-to-all-done.1
  122.2 1.6 reduce.1
  123.9 0.2 reshape.19
  124.2 0.1 copy.22
  124.4 0.3 fusion.2
  124.7 0.1 copy.23.hole
  124.8 40.0 %scatter.1 = f32[64,8,32]{2,1,0:T(8,128)S(1)} custom-call(f32[8,256,256]{2,1,0:T(8,128)S(1)} %ladder.1.part, f32[64,8,32]{2,1,0:T(8,128)S(1)} %copy.23.hole), custom_call_target="tpu_custom_call" | custom-call | tf_op jit(solution)/shard_map/scatter/pallas_call | solution.py:351
  164.9 0.8 copy.24
  (6 shorter events, 0.1 us)
Async XLA Ops:
  0.0 29.4 %copy-start = (f32[48,8,8]{0,2,1:T(8,128)S(1)}, f32[48,8,8]{0,2,1:T(8,128)}, u32[]{:S(2)}) copy-start(f32[48,8,8]{0,2,1:T(8,128)} %param.5) | copy-start | bytes 36868
  0.0 30.1 %copy-start.2 = (f32[2,256,256]{2,1,0:T(8,128)S(1)}, f32[2,256,256]{2,1,0:T(8,128)}, u32[]{:S(2)}) copy-start(f32[2,256,256]{2,1,0:T(8,128)} %amp.1) | copy-start | bytes 1572868
  0.0 30.1 %copy-start.3 = (f32[48,8,256]{2,1,0:T(8,128)S(1)}, f32[48,8,256]{2,1,0:T(8,128)}, u32[]{:S(2)}) copy-start(f32[48,8,256]{2,1,0:T(8,128)} %fac.1) | copy-start | bytes 1179652
  2.3 22.6 %all-to-all-start = ((f32[32,1,512]{2,1,0:T(1,128)}), f32[32,1,512]{2,1,0:T(1,128)S(1)}, u32[]{:S(2)}, u32[]{:S(2)}) async-start(f32[32,1,512]{2,1,0:T(1,128)} %reshape.16), calls=%async_computation | async-start | bytes 131072 | tf_op jit(solution)/shard_map/all_to_all | solution.py:378
  24.9 97.3 %all-to-all-start.1 = ((f32[32,1,512]{2,1,0:T(1,128)}), f32[32,1,512]{2,1,0:T(1,128)}, u32[]{:S(2)}, u32[]{:S(2)}) async-start(f32[32,1,512]{2,1,0:T(1,128)} %reshape.18), calls=%async_computation.1 | async-start | bytes 131072 | tf_op jit(solution)/shard_map/all_to_all | solution.py:379
  74.0 1.7 %copy-start.1 = (f32[12,256,256]{2,1,0:T(8,128)}, f32[12,256,256]{2,1,0:T(8,128)S(1)}, u32[]{:S(2)}) copy-start(f32[12,256,256]{2,1,0:T(8,128)S(1)} %get-tuple-element.7.ball) | copy-start | bytes 9437188

commit v2 on v0

v2 whole, which is shorter than its diff:
```python
import jax
import jax.numpy as jnp
from jax import lax
from jax.experimental import pallas as pl
from jax.experimental.pallas import tpu as pltpu
from jax.sharding import PartitionSpec as P

highest = lax.Precision.HIGHEST
F32 = jnp.float32
BF16 = jnp.bfloat16

Z = 8
K = 4
W = 8
PLANE = K * W
CHIPS = PLANE // 2
OFFSETS = 5
CHUNKS = 6


def remote(src, dst, send_sem, recv_sem, p, w):
    return pltpu.make_async_remote_copy(
        src_ref=src,
        dst_ref=dst,
        send_sem=send_sem,
        recv_sem=recv_sem,
        device_id={"pairs": p, "aux": w},
        device_id_type=pl.DeviceIdType.MESH,
    )


def wait_bytes(ref, sem):
    pltpu.make_async_copy(ref, ref, sem).wait()


def greet(p, w, z, k):
    barrier = pltpu.get_barrier_semaphore()
    m = w * K + k

    def plane_peer(t, c):
        n = lax.rem(m + t, PLANE)
        pl.semaphore_signal(
            barrier, inc=1, device_id={"pairs": z * K + lax.rem(n, K), "aux": n // K},
            device_id_type=pl.DeviceIdType.MESH)
        return c

    def column_peer(t, c):
        pl.semaphore_signal(
            barrier, inc=1, device_id={"pairs": lax.rem(p + t, Z * K), "aux": w},
            device_id_type=pl.DeviceIdType.MESH)
        return c

    lax.fori_loop(1, PLANE, plane_peer, 0)
    lax.fori_loop(1, Z * K, column_peer, 0)
    pl.semaphore_wait(barrier, PLANE + Z * K - 2)


def split(x):
    hi = x.astype(BF16)
    return hi, (x - hi.astype(F32)).astype(BF16)


def dot(a, b):
    return lax.dot_general(a, b, (((1,), (0,)), ((), ())), preferred_element_type=F32)


def dot_t(a, b, precision=None):
    return lax.dot_general(a, b, (((1,), (1,)), ((), ())), preferred_element_type=F32, precision=precision)


def loop(start, stop, body):
    def step(t, c):
        body(t)
        return c

    lax.fori_loop(start, stop, step, 0)


def kernel(amp_hbm, fac, occ, out,
           amp, flip, slots, mine, sall, ball, s_hi, s_lo, b_hi, b_lo, y_hi, y_lo, acc,
           sib, half, parts, tall, at, gb, slot_a, slot_b, hd, hr, occs, gm, cm, hs, hout,
           in_sem, ex_send, ex_recv, a_send, a_recv, s_send, s_recv, w_send, w_recv, ring_send, ring_recv,
           q_send, q_recv, h_send, h_recv, c_send, c_recv, r_send, r_recv, f_send, f_recv, g_send, g_recv):
    p = lax.axis_index("pairs")
    w = lax.axis_index("aux")
    z, k = p // K, lax.rem(p, K)
    core = lax.rem(k, 2)
    m = w * K + k
    chip = w * 2 + k // 2
    other = p + 1 - 2 * core
    virt = amp.shape[1]
    cols = virt // W
    per = ball.shape[0] // CHUNKS
    up = lax.rem(z + 1, Z) * K + k
    down = lax.rem(z + Z - 1, Z) * K + k

    load = pltpu.make_async_copy(amp_hbm, amp, in_sem)
    load.start()
    greet(p, w, z, k)

    def exchange(g, t):
        kk = lax.rem(k + t, K)
        src = fac.at[pl.ds(kk * (per * CHUNKS) + g * per, per)]
        dst = ball.at[pl.ds(g * per, per), pl.ds(pl.multiple_of(8 * p, 8), 8), :]
        if t == 0:
            return pltpu.make_async_copy(src, dst, ex_recv.at[g])
        return remote(src, dst, ex_send.at[g], ex_recv.at[g], z * K + kk, w)

    for g in range(CHUNKS):
        for t in range(K):
            exchange(g, t).start()

    def straight(t):
        kk = lax.rem(k + t, K)
        src = amp.at[:, pl.ds(pl.multiple_of((w * K + kk) * 8, 8), 8), :]
        dst = slots.at[pl.ds(2 * k, 2)]
        if t == 0:
            return pltpu.make_async_copy(src, dst, a_recv)
        return remote(src, dst, a_send, a_recv, z * K + kk, w)

    def turned_far(s, kk):
        src = flip.at[s, pl.ds(pl.multiple_of((w * K + kk) * 8, 8), 8), :]
        return remote(src, slots.at[Z + z], a_send, a_recv, (2 * k + s) * K + kk, w)

    def turned_near(s, kk):
        src = flip.at[s, pl.ds(pl.multiple_of((w * K + kk) * 8, 8), 8), :]
        return pltpu.make_async_copy(src, slots.at[Z + z], a_recv)

    load.wait()
    for t in range(K):
        straight(t).start()
    for s in range(2):
        flip[s] = amp[s].T
    for s in range(2):
        for kk in range(K):
            here = jnp.logical_and(2 * k + s == z, kk == k)
            pl.when(here)(lambda s=s, kk=kk: turned_near(s, kk).start())
            pl.when(jnp.logical_not(here))(lambda s=s, kk=kk: turned_far(s, kk).start())

    def hops(way, g):
        return 4 if (way + g) % 2 == 0 else 3

    def ring(way, g, h):
        origin = lax.rem(z + (Z - h if way == 0 else h), Z)
        part = ball.at[pl.ds(g * per, per), pl.ds(pl.multiple_of(origin * 32, 32), 32), :]
        return remote(part, part, ring_send.at[way, g, h], ring_recv.at[way, g, h], up if way == 0 else down, w)

    def arrive(way, g, h):
        origin = lax.rem(z + (Z - 1 - h if way == 0 else 1 + h), Z)
        part = ball.at[pl.ds(g * per, per), pl.ds(pl.multiple_of(origin * 32, 32), 32), :]
        remote(part, part, ring_send.at[way, g, h], ring_recv.at[way, g, h],
               up if way == 0 else down, w).wait_recv()

    def own(g):
        wait_bytes(ball.at[pl.ds(g * per, per), pl.ds(pl.multiple_of(z * 32, 32), 32), :], ex_recv.at[g])
        for way in range(2):
            ring(way, g, 0).start()

    def forward(g, parity, h):
        for way in range(2):
            if h < hops(way, parity):
                arrive(way, g, h - 1)
                ring(way, g, h).start()

    own(0)
    own(1)

    wait_bytes(slots, a_recv)
    for d in range(OFFSETS):
        j = lax.rem(z + d, Z)
        mine[d] = slots[j] + slots[Z + j]

    def share(t):
        n = lax.rem(chip + t, CHIPS)
        return remote(mine, sall.at[:, chip, core], s_send, s_recv, z * K + lax.rem(n, 2) * 2 + core, n // 2)

    pltpu.make_async_copy(mine, sall.at[:, chip, core], s_recv).start()
    loop(1, CHIPS, lambda t: share(t).start())
    forward(0, 0, 1)

    def occ_share(t):
        return remote(occ, occs.at[w], q_send, q_recv, p, lax.rem(w + t, W))

    pltpu.make_async_copy(occ, occs.at[w], q_recv).start()
    loop(1, W, lambda t: occ_share(t).start())

    at_w = pl.ds(pl.multiple_of(w * cols, cols), cols)
    for s in range(2):
        hd[:, s * cols:(s + 1) * cols] = flip[s, at_w, :].T
        hd[:, (2 + s) * cols:(3 + s) * cols] = amp[s, at_w, :].T
    forward(1, 1, 1)
    forward(0, 0, 2)
    forward(0, 0, 3)

    wait_bytes(sall.at[:, :, core], s_recv)
    across = remote(sall.at[:, :, core], sall.at[:, :, core], w_send, w_recv, other, w)
    across.start()
    acc[...] = jnp.zeros_like(acc)
    wait_bytes(sall.at[:, :, 1 - core], w_recv)
    for d in range(OFFSETS):
        s_hi[d], s_lo[d] = split(sall[d].reshape(virt, virt))

    def first(d):
        bh, bl = b_hi[...], b_lo[...]
        hi, lo = split(dot(bh, s_hi[d]) + dot(bh, s_lo[d]) + dot(bl, s_hi[d]))
        for q in range(per):
            y_hi[q, d * virt:(d + 1) * virt] = hi[q * virt:(q + 1) * virt]
            y_lo[q, d * virt:(d + 1) * virt] = lo[q * virt:(q + 1) * virt]

    def second(q):
        bh, bl = b_hi[q * virt:(q + 1) * virt], b_lo[q * virt:(q + 1) * virt]
        acc[...] += dot_t(y_hi[q], bh) + dot_t(y_hi[q], bl) + dot_t(y_lo[q], bh)

    def chunk_pair(g2):
        for u in range(2):
            g = 2 * g2 + u
            for way in range(2):
                arrive(way, g, hops(way, u) - 1)
            b_hi[...], b_lo[...] = split(ball[pl.ds(g * per, per)].reshape(per * virt, virt))
            pl.when(g + 2 < CHUNKS)(lambda: own(g + 2))
            first(0)
            first(1)
            pl.when(g + 1 < CHUNKS)(lambda: forward(g + 1, 1 - u, 2))
            first(2)
            first(3)
            pl.when(g + 2 < CHUNKS)(lambda: forward(g + 2, u, 1))
            first(4)
            second(0)
            pl.when(g + 1 < CHUNKS)(lambda: forward(g + 1, 1 - u, 3))
            second(1)

    loop(0, CHUNKS // 2, chunk_pair)

    sums = acc.reshape(OFFSETS, CHIPS, 2, 8, virt)
    swap = remote(sums.at[:, :, 1 - core], sib, c_send, c_recv, other, w)
    swap.start()

    def hole_send(t):
        q = lax.rem(p + t, Z * K)
        return remote(hd.at[pl.ds(pl.multiple_of(q * 8, 8), 8), :], hr.at[p], h_send, h_recv, q, w)

    pltpu.make_async_copy(hd.at[pl.ds(pl.multiple_of(p * 8, 8), 8), :], hr.at[p], h_recv).start()
    swap.wait_recv()
    half[...] = sums[:, :, core] + sib[...]

    def spread(t):
        n = lax.rem(chip + t, CHIPS)
        return remote(half.at[:, n], parts.at[chip], r_send, r_recv, z * K + lax.rem(n, 2) * 2 + core, n // 2)

    pltpu.make_async_copy(half.at[:, chip], parts.at[chip], r_recv).start()
    loop(1, CHIPS, lambda t: spread(t).start())
    loop(1, Z * K, lambda t: hole_send(t).start())

    wait_bytes(occs, q_recv)
    g_sum = dot_t(occs[0], occs[0], highest)
    for n in range(1, W):
        g_sum = g_sum + dot_t(occs[n], occs[n], highest)
    gm[...] = g_sum
    by_k = [gm[pl.ds(kk, 8, stride=8), :] for kk in range(8)]
    for j in range(8):
        cm[pl.ds(j, 8, stride=8), :] = jnp.concatenate([x[:, j * 8:j * 8 + 8] for x in by_k], axis=1)
    wait_bytes(hr, h_recv)
    flat = hr.reshape(Z * K * 8, 4 * cols)
    by_a = [flat[pl.ds(a, Z * K, stride=8), :] for a in range(8)]
    for s in range(2):
        for e in range(2):
            hs[e, pl.ds(s, Z * K, stride=2), :] = jnp.concatenate(
                [x[:, s * cols:(s + 1) * cols] for x in by_a[4 * e:4 * e + 4]], axis=1)
    for l2 in range(4):
        by_a = [flat[pl.ds(8 * l2 + a, 8, stride=32), :] for a in range(8)]
        for s in range(2):
            for e in range(2):
                at_row = 16 * l2 + 8 * s
                hs[e, at_row:at_row + 8, :] += jnp.concatenate(
                    [x[:, (2 + s) * cols:(3 + s) * cols] for x in by_a[4 * e:4 * e + 4]], axis=1)
    hole = [lax.dot_general(cm[...], hs[e], (((1,), (0,)), ((), ())), preferred_element_type=F32, precision=highest)
            for e in range(2)]
    for a in range(8):
        hout[pl.ds(a, 64, stride=8), :] = hole[a // 4][:, a % 4 * cols:(a % 4 + 1) * cols]

    wait_bytes(parts, r_recv)
    total = parts[0]
    for n in range(1, CHIPS):
        total = total + parts[n]
    tall[...] = jnp.zeros_like(tall)
    for d in range(4):
        tall[pl.ds(pl.multiple_of(d * 32 + 8 * k, 8), 8), :] = total[d]
    at[...] = tall[...].T
    for ww in range(W):
        for d in range(1, OFFSETS):
            gb[ww, :, (d - 1) * cols:d * cols] = total[d][:, ww * cols:(ww + 1) * cols]

    def col_send(t):
        q = lax.rem(p + t, Z * K)
        return remote(at.at[pl.ds(pl.multiple_of(q * 8, 8), 8), :], slot_a.at[p], f_send, f_recv, q, w)

    def row_send(ww):
        return remote(gb.at[ww], slot_b.at[z], g_send, g_recv, m, ww)

    def row_here(ww):
        return jnp.logical_and(m == p, ww == w)

    for ww in range(W):
        pl.when(row_here(ww))(lambda ww=ww: pltpu.make_async_copy(gb.at[ww], slot_b.at[z], g_recv).start())
        pl.when(jnp.logical_not(row_here(ww)))(lambda ww=ww: row_send(ww).start())
    pltpu.make_async_copy(at.at[pl.ds(pl.multiple_of(p * 8, 8), 8), :], slot_a.at[p], f_recv).start()
    loop(1, Z * K, lambda t: col_send(t).start())

    wait_bytes(slot_b, g_recv)
    for zz in range(Z):
        tile = slot_b[zz]
        for d in range(1, OFFSETS):
            pair = zz * 8 + (zz + d) % 8
            out[pair] = tile[:, (d - 1) * cols:d * cols] + hout[pair * 8:pair * 8 + 8, :]
    wait_bytes(slot_a, f_recv)
    for zz in range(Z):
        tile = slot_a[zz * K] + slot_a[zz * K + 1] + slot_a[zz * K + 2] + slot_a[zz * K + 3]
        for d in range(4):
            pair = (zz + d) % 8 * 8 + zz
            out[pair] = tile[:, d * cols:(d + 1) * cols] + hout[pair * 8:pair * 8 + 8, :]

    for g in range(CHUNKS):
        for t in range(1, K):
            exchange(g, t).wait_send()
        for way in range(2):
            for h in range(hops(way, g)):
                ring(way, g, h).wait_send()
    for t in range(1, K):
        straight(t).wait_send()
    for s in range(2):
        for kk in range(K):
            here = jnp.logical_and(2 * k + s == z, kk == k)
            pl.when(jnp.logical_not(here))(lambda s=s, kk=kk: turned_far(s, kk).wait_send())
    across.wait_send()
    swap.wait_send()
    for ww in range(W):
        pl.when(jnp.logical_not(row_here(ww)))(lambda ww=ww: row_send(ww).wait_send())
    wait_bytes(parts.at[pl.ds(0, CHIPS - 1)], s_send)
    wait_bytes(parts.at[pl.ds(0, CHIPS - 1)], r_send)
    wait_bytes(occs.at[pl.ds(0, W - 1)], q_send)
    wait_bytes(hr.at[pl.ds(0, Z * K - 1)], h_send)
    wait_bytes(slot_a.at[pl.ds(0, Z * K - 1)], f_send)


def shards(amplitudes, factors, occ_factors):
    aux_local, rows, virt = factors.shape
    occupied = occ_factors.shape[1]
    local = aux_local // K
    per = local // CHUNKS
    cols = virt // W
    occ = occ_factors.transpose(1, 2, 0).reshape(occupied * occupied, aux_local)
    vm = pl.BlockSpec(memory_space=pltpu.VMEM)
    anywhere = pl.BlockSpec(memory_space=pltpu.HBM)
    dma = pltpu.SemaphoreType.DMA
    v = pltpu.VMEM
    scratch = [
        v((2, virt, virt), F32), v((2, virt, virt), F32),
        v((2 * Z, 8, virt), F32), v((OFFSETS, 8, virt), F32),
        v((OFFSETS, CHIPS, 2, 8, virt), F32), v((local, virt, virt), F32),
        v((OFFSETS, virt, virt), BF16), v((OFFSETS, virt, virt), BF16),
        v((per * virt, virt), BF16), v((per * virt, virt), BF16),
        v((per, OFFSETS * virt, virt), BF16), v((per, OFFSETS * virt, virt), BF16),
        v((OFFSETS * virt, virt), F32),
        v((OFFSETS, CHIPS, 8, virt), F32), v((OFFSETS, CHIPS, 8, virt), F32),
        v((CHIPS, OFFSETS, 8, virt), F32),
        v((128, virt), F32), v((virt, 128), F32),
        v((W, 8, 128), F32), v((Z * K, 8, 128), F32), v((Z, 8, 128), F32),
        v((virt, 128), F32), v((Z * K, 8, 128), F32),
        v((W, occupied * occupied, aux_local), F32),
        v((64, 64), F32), v((64, 64), F32), v((2, 64, 128), F32), v((64 * 8, cols), F32),
        dma(()), dma((CHUNKS,)), dma((CHUNKS,)),
        dma(()), dma(()), dma(()), dma(()), dma(()), dma(()),
        dma((2, CHUNKS, 4)), dma((2, CHUNKS, 4)),
        dma(()), dma(()), dma(()), dma(()), dma(()), dma(()), dma(()), dma(()), dma(()), dma(()), dma(()), dma(()),
    ]
    return pl.pallas_call(
        kernel,
        out_shape=jax.ShapeDtypeStruct((occupied * occupied, rows, cols), F32),
        in_specs=[anywhere, anywhere, vm],
        out_specs=vm,
        scratch_shapes=scratch,
        compiler_params=pltpu.CompilerParams(
            collective_id=0, has_side_effects=True, vmem_limit_bytes=52 << 20),
        name="residual",
    )(amplitudes, factors, occ)


def solution(mesh):
    placed = (P("pairs", None, None), P("aux", "pairs", None), P("aux", None, None))
    return jax.shard_map(
        shards, mesh=mesh, in_specs=placed, out_specs=P(None, "pairs", "aux"), check_vma=False
    )
```

time: 1200 us -> 109 us (0.09)
  blocking collectives: 984 us -> 0 us
  Pallas kernels: 0 us -> 105 us
  matrix products: 56.4 us -> 0 us
  waiting for transfers between devices: 44.8 us -> 0 us
  local copies, waits for them, and re-layouts: 44.5 us -> 3.59 us
  starting transfers between devices: 29.1 us -> 0 us
  loops' own time: 17.9 us -> 0 us
  between operations: 13.7 us -> 0.01 us
    all_gather x24 -> x0, blocking collectives: 957 us -> none  [whole_step(): whole_rows = lax.all_gather(row_block, 'pairs', axis=1, tiled=True)]
    pallas_call x0 -> x1, Pallas kernels: none -> 105 us  [shards(): pl.pallas_call(kernel, out_shape=jax.ShapeDtypeStruct((occupied * occupie...]
    dot_general x49 -> x0, matrix products: 55.8 us -> none  [the longest x24 30.3 us: both_sides(): jnp.einsum('pac,picb->iab', row_block, mixed_terms, precision=highest)]
    dynamic_slice x50 -> x0, local copies, waits for them, and re-layouts: 33.5 us -> none  [the longest x24 17.4 us: whole_step(): row_block = lax.dynamic_slice_in_dim(factors, block_index * 2, 2, 0)]
    all_to_all x4 -> x0, starting transfers between devices: 29.1 us -> none  [the longest x1 15.2 us: shards(): lax.all_to_all(part_flip, 'pairs', split_axis=1, concat_axis=0, tiled=True)]
    psum x1 -> x0, blocking collectives: 26.1 us -> none  [shards(): particle, coupling = lax.psum((particle, coupling), 'aux')]
    psum x1 -> x0, waiting for transfers between devices: 22.7 us -> none  [shards(): particle, coupling = lax.psum((particle, coupling), 'aux')]
    all_to_all x4 -> x0, waiting for transfers between devices: 22.1 us -> none  [the longest x1 8.16 us: shards(): lax.all_to_all(part_cols, 'pairs', split_axis=1, concat_axis=0, tiled=True)]
  transfers between devices with their start and end apart: 5 -> 0, of which waited for: 4 -> 0; matrix products, arithmetic and copies ran while one was open for 1% -> 0% of each run, Pallas kernels for 0% -> 0%
where the time goes in v2:
time: 109 us; the launch traced here: 108 us
  Pallas kernels  105 us (96%)
  local copies, waits for them, and re-layouts  3.59 us (3%)
    pallas_call x1, Pallas kernels, shards(): pl.pallas_call(kernel, out_shape=jax.ShapeDtypeStruct((occupied * occupie...  105 us
    unnamed x6, local copies, waits for them, and re-layouts  2.79 us

profile of v2, /device:TPU:1, one launch (start us, length us, event | category | flops | bytes accessed | tf_op | source)
XLA Modules:
  0.0 108.4 jit_solution(5653453210593336571)
XLA Ops:
  0.0 0.0 copy-start
  0.0 1.0 copy-done
  1.0 0.0 copy-start.1
  1.0 1.0 copy-done.1
  2.0 0.0 copy-start.2
  2.0 0.8 copy-done.2
  2.8 104.8 %residual.1 = f32[64,8,32]{2,1,0:T(8,128)S(1)} custom-call(f32[2,256,256]{2,1,0:T(8,128)S(1)} %copy-done, f32[48,8,256]{2,1,0:T(8,128)S(1)} %copy-done.1, f32[64,48]{1,0:T(8,128)S(1)} %bitcast.3), custom_call_target="tpu_custom_call" | custom-call | tf_op jit(solution)/shard_map/residual/pallas_call | solution.py:376
  107.6 0.8 copy.4
Async XLA Ops:
  0.0 1.0 copy-start
  1.0 1.0 copy-start.1
  2.0 0.8 copy-start.2

commit v3 on v2

v3 whole, which is shorter than its diff:
```python
import jax
import jax.numpy as jnp
from jax import lax
from jax.experimental import pallas as pl
from jax.experimental.pallas import tpu as pltpu
from jax.sharding import PartitionSpec as P

highest = lax.Precision.HIGHEST
F32 = jnp.float32
BF16 = jnp.bfloat16

Z = 8
K = 4
W = 8
PLANE = K * W
CHIPS = PLANE // 2
OFFSETS = 5
GROUPS = ((0, 6), (6, 6))


def remote(src, dst, send_sem, recv_sem, p, w):
    return pltpu.make_async_remote_copy(
        src_ref=src,
        dst_ref=dst,
        send_sem=send_sem,
        recv_sem=recv_sem,
        device_id={"pairs": p, "aux": w},
        device_id_type=pl.DeviceIdType.MESH,
    )


def wait_bytes(ref, sem):
    pltpu.make_async_copy(ref, ref, sem).wait()


def greet(p, w, z, core, chip):
    barrier = pltpu.get_barrier_semaphore()

    def plane_peer(t):
        n = lax.rem(chip + t, CHIPS)
        pl.semaphore_signal(
            barrier, inc=1, device_id={"pairs": z * K + lax.rem(n, 2) * 2 + core, "aux": n // 2},
            device_id_type=pl.DeviceIdType.MESH)

    def column_peer(t):
        pl.semaphore_signal(
            barrier, inc=1, device_id={"pairs": lax.rem(p + t, Z * K), "aux": w},
            device_id_type=pl.DeviceIdType.MESH)

    loop(1, CHIPS, plane_peer)
    loop(1, Z * K, column_peer)


def met():
    pl.semaphore_wait(pltpu.get_barrier_semaphore(), CHIPS + Z * K - 2)


def loop(start, stop, body):
    def step(t, c):
        body(t)
        return c

    lax.fori_loop(start, stop, step, 0)


def split(x):
    hi = x.astype(BF16)
    return hi, (x - hi.astype(F32)).astype(BF16)


def dot(a, b):
    return lax.dot_general(a, b, (((1,), (0,)), ((), ())), preferred_element_type=F32)


def dot_t(a, b, precision=None):
    return lax.dot_general(a, b, (((1,), (1,)), ((), ())), preferred_element_type=F32, precision=precision)


def kernel(amp_hbm, fac, occ, out,
           amp, flip, slots, mine, sall, ball, s3, b3, y3, acc,
           sib, half, parts, tall, at, gb, slot_a, slot_b, hd, hr, occs, gm, cm, hs, hout,
           in_sem, ex_send, ex_recv, a_send, a_recv, s_send, s_recv, w_send, w_recv, l_send, ring_send, ring_recv,
           q_send, q_recv, h_send, h_recv, c_send, c_recv, r_send, r_recv, f_send, f_recv, g_send, g_recv):
    p = lax.axis_index("pairs")
    w = lax.axis_index("aux")
    z, k = p // K, lax.rem(p, K)
    core = lax.rem(k, 2)
    m = w * K + k
    chip = w * 2 + k // 2
    other = p + 1 - 2 * core
    virt = amp.shape[1]
    cols = virt // W
    local = ball.shape[0]
    half_of = k // 2

    load = pltpu.make_async_copy(amp_hbm, amp, in_sem)
    load.start()
    greet(p, w, z, core, chip)
    met()

    def mine_of(gi, kk):
        return fac.at[pl.ds(kk * ball.shape[0] + GROUPS[gi][0], GROUPS[gi][1])]

    def my_rows(gi):
        return ball.at[pl.ds(*GROUPS[gi]), pl.ds(pl.multiple_of(8 * p, 8), 8), :]

    def region(gi, part, origin):
        row = origin * 32 + (half_of if part == 0 else 1 - half_of) * 16
        return ball.at[pl.ds(*GROUPS[gi]), pl.ds(pl.multiple_of(row, 16), 16), :]

    def keep(gi):
        return pltpu.make_async_copy(mine_of(gi, k), my_rows(gi), ex_recv.at[gi, 0])

    def exchange(gi, t):
        kk = lax.rem(half_of + t // 2, 2) * 2 + lax.rem(core + t, 2)
        return remote(mine_of(gi, kk), my_rows(gi), ex_send.at[gi, t], ex_recv.at[gi, t // 2], z * K + kk, w)

    def neighbour(way):
        return lax.rem(z + (1 if way == 0 else Z - 1), Z) * K

    def hops(way, gi, part):
        return 4 - (way + gi + part) % 2

    def launch(way, gi, t):
        kk = half_of * 2 + lax.rem(core + t, 2)
        return remote(mine_of(gi, kk), my_rows(gi), l_send.at[way, gi, t], ring_recv.at[way, gi, 0, 0],
                      neighbour(way) + kk, w)

    def ring(way, gi, part, h):
        here = region(gi, part, lax.rem(z + (Z - h if way == 0 else h), Z))
        return remote(here, here, ring_send.at[way, gi, part, h], ring_recv.at[way, gi, part, h],
                      neighbour(way) + k, w)

    def arrive(way, gi, part, h):
        here = region(gi, part, lax.rem(z + (Z - 1 - h if way == 0 else 1 + h), Z))
        remote(here, here, ring_send.at[way, gi, part, h], ring_recv.at[way, gi, part, h],
               neighbour(way) + k, w).wait_recv()

    def begin(gi):
        for way in range(2):
            for t in range(2):
                launch(way, gi, t).start()
        keep(gi).start()
        for t in range(1, K):
            exchange(gi, t).start()

    def begin_far(gi):
        wait_bytes(region(gi, 1, z), ex_recv.at[gi, 1])
        for way in range(2):
            ring(way, gi, 1, 0).start()

    def forward(gi, part, h):
        for way in range(2):
            if h < hops(way, gi, part):
                arrive(way, gi, part, h - 1)
                ring(way, gi, part, h).start()

    def landed(h):
        for gi in range(2):
            for part in range(2):
                for way in range(2):
                    if hops(way, gi, part) == h + 1:
                        arrive(way, gi, part, h)

    begin(0)
    begin(1)

    def straight(t):
        kk = lax.rem(k + t, K)
        src = amp.at[:, pl.ds(pl.multiple_of((w * K + kk) * 8, 8), 8), :]
        dst = slots.at[pl.ds(2 * k, 2)]
        if t == 0:
            return pltpu.make_async_copy(src, dst, a_recv)
        return remote(src, dst, a_send, a_recv, z * K + kk, w)

    def turned_far(s, kk):
        src = flip.at[s, pl.ds(pl.multiple_of((w * K + kk) * 8, 8), 8), :]
        return remote(src, slots.at[Z + z], a_send, a_recv, (2 * k + s) * K + kk, w)

    def turned_near(s, kk):
        src = flip.at[s, pl.ds(pl.multiple_of((w * K + kk) * 8, 8), 8), :]
        return pltpu.make_async_copy(src, slots.at[Z + z], a_recv)

    load.wait()
    for s in range(2):
        flip[s] = amp[s].T
    for s in range(2):
        for kk in range(K):
            here = jnp.logical_and(2 * k + s == z, kk == k)
            pl.when(here)(lambda s=s, kk=kk: turned_near(s, kk).start())
            pl.when(jnp.logical_not(here))(lambda s=s, kk=kk: turned_far(s, kk).start())
    for t in range(K):
        straight(t).start()
    begin_far(0)
    begin_far(1)

    def share(t):
        n = lax.rem(chip + t, CHIPS)
        return remote(mine, sall.at[:, chip, core], s_send, s_recv, z * K + lax.rem(n, 2) * 2 + core, n // 2)

    wait_bytes(slots, a_recv)
    for d in range(OFFSETS):
        j = lax.rem(z + d, Z)
        mine[d] = slots[j] + slots[Z + j]
    pltpu.make_async_copy(mine, sall.at[:, chip, core], s_recv).start()
    loop(1, CHIPS, lambda t: share(t).start())
    for part in range(2):
        for gi in range(2):
            forward(gi, part, 1)

    def occ_share(t):
        return remote(occ, occs.at[w], q_send, q_recv, p, lax.rem(w + t, W))

    pltpu.make_async_copy(occ, occs.at[w], q_recv).start()
    loop(1, W, lambda t: occ_share(t).start())
    at_w = pl.ds(pl.multiple_of(w * cols, cols), cols)
    for s in range(2):
        hd[:, s * cols:(s + 1) * cols] = flip[s, at_w, :].T
        hd[:, (2 + s) * cols:(3 + s) * cols] = amp[s, at_w, :].T
    forward(0, 0, 2)
    forward(1, 0, 2)
    wait_bytes(sall.at[:, :, core], s_recv)
    across = remote(sall.at[:, :, core], sall.at[:, :, core], w_send, w_recv, other, w)
    across.start()
    forward(0, 1, 2)
    forward(1, 1, 2)

    wait_bytes(occs, q_recv)
    g_sum = dot_t(occs[0], occs[0], highest)
    for n in range(1, W):
        g_sum = g_sum + dot_t(occs[n], occs[n], highest)
    gm[...] = g_sum
    by_k = [gm[pl.ds(kk, 8, stride=8), :] for kk in range(8)]
    for j in range(8):
        cm[pl.ds(j, 8, stride=8), :] = jnp.concatenate([x[:, j * 8:j * 8 + 8] for x in by_k], axis=1)

    wait_bytes(sall.at[:, :, 1 - core], w_recv)
    for d in range(OFFSETS):
        hi, lo = split(sall[d].reshape(virt, virt))
        s3[d, :virt], s3[d, virt:2 * virt], s3[d, 2 * virt:] = hi, lo, hi

    def first(origin):
        rows = pl.ds(pl.multiple_of(origin * 32, 32), 32)
        hi, lo = split(ball[:, rows, :])
        b3[:, rows, :virt], b3[:, rows, virt:2 * virt], b3[:, rows, 2 * virt:] = hi, hi, lo

        def one(d):
            y_hi, y_lo = split(dot(b3[:, rows, :].reshape(local * 32, 3 * virt), s3[d]))
            for q in range(local):
                at_q = q * 3 * virt
                y3[d, rows, at_q:at_q + virt] = y_hi[q * 32:(q + 1) * 32]
                y3[d, rows, at_q + virt:at_q + 2 * virt] = y_lo[q * 32:(q + 1) * 32]
                y3[d, rows, at_q + 2 * virt:at_q + 3 * virt] = y_hi[q * 32:(q + 1) * 32]

        loop(0, OFFSETS, one)

    def both(step):
        loop(0, 2, lambda t: first(lax.rem(z + step + t * (Z - 2 * step), Z)))

    def second(d):
        term = None
        for q in range(local):
            x = dot_t(y3[d, :, q * 3 * virt:(q + 1) * 3 * virt], b3[q])
            term = x if term is None else term + x
        acc[pl.ds(pl.multiple_of(d * virt, virt), virt)] = term

    sums = acc.reshape(OFFSETS, CHIPS, 2, 8, virt)

    def swap(d):
        return remote(sums.at[d, :, 1 - core], sib.at[d], c_send.at[d], c_recv.at[d], other, w)

    for gi in range(2):
        wait_bytes(region(gi, 0, z), ex_recv.at[gi, 0])
    first(z)
    forward(0, 0, 3)
    both(1)
    forward(1, 0, 3)
    both(2)
    forward(0, 1, 3)
    forward(1, 1, 3)
    landed(2)
    both(3)
    landed(3)
    first(lax.rem(z + 4, Z))

    def hole_send(t):
        q = lax.rem(p + t, Z * K)
        return remote(hd.at[pl.ds(pl.multiple_of(q * 8, 8), 8), :], hr.at[p], h_send, h_recv, q, w)

    groups = ((0, 3), (3, 5))

    def spread(t, e):
        n = lax.rem(chip + t, CHIPS)
        ds = pl.ds(groups[e][0], groups[e][1] - groups[e][0])
        return remote(half.at[ds, n], parts.at[chip, ds], r_send, r_recv, z * K + lax.rem(n, 2) * 2 + core, n // 2)

    def spread_group(e):
        low, high = groups[e]
        for d in range(low, high):
            swap(d).wait_recv()
            half[d] = sums[d, :, core] + sib[d]
        ds = pl.ds(low, high - low)
        pltpu.make_async_copy(half.at[ds, chip], parts.at[chip, ds], r_recv).start()
        loop(1, CHIPS, lambda t: spread(t, e).start())

    def finish(d):
        second(d)
        swap(d).start()
        pl.when(d == groups[0][1])(lambda: spread_group(0))

    loop(0, OFFSETS, finish)
    pltpu.make_async_copy(hd.at[pl.ds(pl.multiple_of(p * 8, 8), 8), :], hr.at[p], h_recv).start()
    spread_group(1)
    loop(1, Z * K, lambda t: hole_send(t).start())

    wait_bytes(hr, h_recv)
    flat = hr.reshape(Z * K * 8, 4 * cols)
    by_a = [flat[pl.ds(a, Z * K, stride=8), :] for a in range(8)]
    for s in range(2):
        for e in range(2):
            hs[e, pl.ds(s, Z * K, stride=2), :] = jnp.concatenate(
                [x[:, s * cols:(s + 1) * cols] for x in by_a[4 * e:4 * e + 4]], axis=1)
    for l2 in range(4):
        by_a = [flat[pl.ds(8 * l2 + a, 8, stride=32), :] for a in range(8)]
        for s in range(2):
            for e in range(2):
                at_row = 16 * l2 + 8 * s
                hs[e, at_row:at_row + 8, :] += jnp.concatenate(
                    [x[:, (2 + s) * cols:(3 + s) * cols] for x in by_a[4 * e:4 * e + 4]], axis=1)
    hole = [lax.dot_general(cm[...], hs[e], (((1,), (0,)), ((), ())), preferred_element_type=F32, precision=highest)
            for e in range(2)]
    for a in range(8):
        hout[pl.ds(a, 64, stride=8), :] = hole[a // 4][:, a % 4 * cols:(a % 4 + 1) * cols]

    wait_bytes(parts, r_recv)
    total = parts[0]
    for n in range(1, CHIPS):
        total = total + parts[n]
    tall[...] = jnp.zeros_like(tall)
    for d in range(4):
        tall[pl.ds(pl.multiple_of(d * 32 + 8 * k, 8), 8), :] = total[d]
    at[...] = tall[...].T
    for ww in range(W):
        for d in range(1, OFFSETS):
            gb[ww, :, (d - 1) * cols:d * cols] = total[d][:, ww * cols:(ww + 1) * cols]

    def col_send(t):
        q = lax.rem(p + t, Z * K)
        return remote(at.at[pl.ds(pl.multiple_of(q * 8, 8), 8), :], slot_a.at[p], f_send, f_recv, q, w)

    def row_send(ww):
        return remote(gb.at[ww], slot_b.at[z], g_send, g_recv, m, ww)

    def row_here(ww):
        return jnp.logical_and(m == p, ww == w)

    for ww in range(W):
        pl.when(row_here(ww))(lambda ww=ww: pltpu.make_async_copy(gb.at[ww], slot_b.at[z], g_recv).start())
        pl.when(jnp.logical_not(row_here(ww)))(lambda ww=ww: row_send(ww).start())
    pltpu.make_async_copy(at.at[pl.ds(pl.multiple_of(p * 8, 8), 8), :], slot_a.at[p], f_recv).start()
    loop(1, Z * K, lambda t: col_send(t).start())

    wait_bytes(slot_b, g_recv)
    for zz in range(Z):
        tile = slot_b[zz]
        for d in range(1, OFFSETS):
            pair = zz * 8 + (zz + d) % 8
            out[pair] = tile[:, (d - 1) * cols:d * cols] + hout[pair * 8:pair * 8 + 8, :]
    wait_bytes(slot_a, f_recv)
    for zz in range(Z):
        tile = slot_a[zz * K] + slot_a[zz * K + 1] + slot_a[zz * K + 2] + slot_a[zz * K + 3]
        for d in range(4):
            pair = (zz + d) % 8 * 8 + zz
            out[pair] = tile[:, d * cols:(d + 1) * cols] + hout[pair * 8:pair * 8 + 8, :]

    for gi in range(len(GROUPS)):
        for t in range(1, K):
            exchange(gi, t).wait_send()
        for way in range(2):
            for t in range(2):
                launch(way, gi, t).wait_send()
            for part in range(2):
                for h in range(1 - part, hops(way, gi, part)):
                    ring(way, gi, part, h).wait_send()
    for t in range(1, K):
        straight(t).wait_send()
    for s in range(2):
        for kk in range(K):
            here = jnp.logical_and(2 * k + s == z, kk == k)
            pl.when(jnp.logical_not(here))(lambda s=s, kk=kk: turned_far(s, kk).wait_send())
    across.wait_send()
    for d in range(OFFSETS):
        swap(d).wait_send()
    for ww in range(W):
        pl.when(jnp.logical_not(row_here(ww)))(lambda ww=ww: row_send(ww).wait_send())
    wait_bytes(parts.at[pl.ds(0, CHIPS - 1)], s_send)
    wait_bytes(parts.at[pl.ds(0, CHIPS - 1)], r_send)
    wait_bytes(occs.at[pl.ds(0, W - 1)], q_send)
    wait_bytes(hr.at[pl.ds(0, Z * K - 1)], h_send)
    wait_bytes(slot_a.at[pl.ds(0, Z * K - 1)], f_send)


def shards(amplitudes, factors, occ_factors):
    aux_local, rows, virt = factors.shape
    occupied = occ_factors.shape[1]
    local = aux_local // K
    cols = virt // W
    occ = occ_factors.transpose(1, 2, 0).reshape(occupied * occupied, aux_local)
    vm = pl.BlockSpec(memory_space=pltpu.VMEM)
    anywhere = pl.BlockSpec(memory_space=pltpu.HBM)
    dma = pltpu.SemaphoreType.DMA
    v = pltpu.VMEM
    scratch = [
        v((2, virt, virt), F32), v((2, virt, virt), F32),
        v((2 * Z, 8, virt), F32), v((OFFSETS, 8, virt), F32),
        v((OFFSETS, CHIPS, 2, 8, virt), F32), v((local, virt, virt), F32),
        v((OFFSETS, 3 * virt, virt), BF16), v((local, virt, 3 * virt), BF16),
        v((OFFSETS, virt, local * 3 * virt), BF16),
        v((OFFSETS * virt, virt), F32),
        v((OFFSETS, CHIPS, 8, virt), F32), v((OFFSETS, CHIPS, 8, virt), F32),
        v((CHIPS, OFFSETS, 8, virt), F32),
        v((128, virt), F32), v((virt, 128), F32),
        v((W, 8, 128), F32), v((Z * K, 8, 128), F32), v((Z, 8, 128), F32),
        v((virt, 128), F32), v((Z * K, 8, 128), F32),
        v((W, occupied * occupied, aux_local), F32),
        v((64, 64), F32), v((64, 64), F32), v((2, 64, 128), F32), v((64 * 8, cols), F32),
        dma(()), dma((len(GROUPS), K)), dma((len(GROUPS), 2)),
        dma(()), dma(()), dma(()), dma(()), dma(()), dma(()),
        dma((2, len(GROUPS), 2)), dma((2, len(GROUPS), 2, 4)), dma((2, len(GROUPS), 2, 4)),
        dma(()), dma(()), dma(()), dma(()), dma((OFFSETS,)), dma((OFFSETS,)), dma(()), dma(()), dma(()), dma(()), dma(()), dma(()),
    ]
    return pl.pallas_call(
        kernel,
        out_shape=jax.ShapeDtypeStruct((occupied * occupied, rows, cols), F32),
        in_specs=[anywhere, anywhere, vm],
        out_specs=vm,
        scratch_shapes=scratch,
        compiler_params=pltpu.CompilerParams(
            collective_id=0, has_side_effects=True, vmem_limit_bytes=(64 << 20) - (330 << 10)),
        name="residual",
    )(amplitudes, factors, occ)


def solution(mesh):
    placed = (P("pairs", None, None), P("aux", "pairs", None), P("aux", None, None))
    return jax.shard_map(
        shards, mesh=mesh, in_specs=placed, out_specs=P(None, "pairs", "aux"), check_vma=False
    )
```

time: 109 us -> 82.2 us (0.75)
  Pallas kernels: 105 us -> 80.3 us
  local copies, waits for them, and re-layouts: 3.59 us -> 1.73 us
    pallas_call x1, Pallas kernels: 105 us -> 80.3 us  [shards(): pl.pallas_call(kernel, out_shape=jax.ShapeDtypeStruct((occupied * occupie...]
    unnamed x6 -> x0, local copies, waits for them, and re-layouts: 2.79 us -> none
where the time goes in v3:
time: 82.2 us; the launch traced here: 82 us
  Pallas kernels  80.3 us (98%)
  local copies, waits for them, and re-layouts  1.73 us (2%)
    pallas_call x1, Pallas kernels, shards(): pl.pallas_call(kernel, out_shape=jax.ShapeDtypeStruct((occupied * occupie...  80.3 us
    pallas_call x1, local copies, waits for them, and re-layouts, shards(): pl.pallas_call(kernel, out_shape=jax.ShapeDtypeStruct((occupied * occupie...  1.73 us

profile of v3, /device:TPU:1, one launch (start us, length us, event | category | flops | bytes accessed | tf_op | source)
XLA Modules:
  0.0 82.0 jit_solution(164911371255825415)
XLA Ops:
  0.0 80.3 %residual.1 = f32[64,8,32]{2,1,0:T(8,128)} custom-call(f32[2,256,256]{2,1,0:T(8,128)} %amp_hbm.1, f32[48,8,256]{2,1,0:T(8,128)} %fac.1, f32[64,48]{1,0:T(8,128)} %bitcast.3), custom_call_target="tpu_custom_call" | custom-call | tf_op jit(solution)/shard_map/residual/pallas_call | solution.py:432
  80.3 1.7 %copy.4 = f32[64,8,32]{0,2,1:T(8,128)} copy(f32[64,8,32]{2,1,0:T(8,128)} %residual.1) | data formatting | bytes 131072 | tf_op jit(solution)/shard_map/residual/pallas_call | solution.py:432

commit v4 on v3

--- a/solution.py
+++ b/solution.py
@@ -16,6 +16,9 @@
 CHIPS = PLANE // 2
 OFFSETS = 5
 GROUPS = ((0, 6), (6, 6))
+
+
+SUMS = ((0, 2), (2, 4), (4, 5))
 
 
 def remote(src, dst, send_sem, recv_sem, p, w):
@@ -78,7 +81,7 @@
 
 def kernel(amp_hbm, fac, occ, out,
            amp, flip, slots, mine, sall, ball, s3, b3, y3, acc,
-           sib, half, parts, tall, at, gb, slot_a, slot_b, hd, hr, occs, gm, cm, hs, hout,
+           sib, half, parts, tall, at, gb, gb4, slot_a, slot_b, slot_b4, hd, hr, occs, gm, cm, hs, hout,
            in_sem, ex_send, ex_recv, a_send, a_recv, s_send, s_recv, w_send, w_recv, l_send, ring_send, ring_recv,
            q_send, q_recv, h_send, h_recv, c_send, c_recv, r_send, r_recv, f_send, f_recv, g_send, g_recv):
     p = lax.axis_index("pairs")
@@ -156,14 +159,14 @@
                 ring(way, gi, part, h).start()
 
     def landed(h):
-        for gi in range(2):
+        for gi in range(len(GROUPS)):
             for part in range(2):
                 for way in range(2):
                     if hops(way, gi, part) == h + 1:
                         arrive(way, gi, part, h)
 
-    begin(0)
-    begin(1)
+    for gi in range(len(GROUPS)):
+        begin(gi)
 
     def straight(t):
         kk = lax.rem(k + t, K)
@@ -191,8 +194,8 @@
             pl.when(jnp.logical_not(here))(lambda s=s, kk=kk: turned_far(s, kk).start())
     for t in range(K):
         straight(t).start()
-    begin_far(0)
-    begin_far(1)
+    for gi in range(len(GROUPS)):
+        begin_far(gi)
 
     def share(t):
         n = lax.rem(chip + t, CHIPS)
@@ -205,7 +208,7 @@
     pltpu.make_async_copy(mine, sall.at[:, chip, core], s_recv).start()
     loop(1, CHIPS, lambda t: share(t).start())
     for part in range(2):
-        for gi in range(2):
+        for gi in range(len(GROUPS)):
             forward(gi, part, 1)
 
     def occ_share(t):
@@ -217,13 +220,13 @@
     for s in range(2):
         hd[:, s * cols:(s + 1) * cols] = flip[s, at_w, :].T
         hd[:, (2 + s) * cols:(3 + s) * cols] = amp[s, at_w, :].T
-    forward(0, 0, 2)
-    forward(1, 0, 2)
+    for gi in range(len(GROUPS)):
+        forward(gi, 0, 2)
     wait_bytes(sall.at[:, :, core], s_recv)
     across = remote(sall.at[:, :, core], sall.at[:, :, core], w_send, w_recv, other, w)
     across.start()
-    forward(0, 1, 2)
-    forward(1, 1, 2)
+    for gi in range(len(GROUPS)):
+        forward(gi, 1, 2)
 
     wait_bytes(occs, q_recv)
     g_sum = dot_t(occs[0], occs[0], highest)
@@ -269,50 +272,52 @@
     def swap(d):
         return remote(sums.at[d, :, 1 - core], sib.at[d], c_send.at[d], c_recv.at[d], other, w)
 
-    for gi in range(2):
+    for gi in range(len(GROUPS)):
         wait_bytes(region(gi, 0, z), ex_recv.at[gi, 0])
     first(z)
-    forward(0, 0, 3)
+    late = [(gi, part) for part in range(2) for gi in range(len(GROUPS))]
+    share_of = len(late) // 4
+    for gi, part in late[:share_of]:
+        forward(gi, part, 3)
     both(1)
-    forward(1, 0, 3)
+    for gi, part in late[share_of:2 * share_of]:
+        forward(gi, part, 3)
     both(2)
-    forward(0, 1, 3)
-    forward(1, 1, 3)
+    for gi, part in late[2 * share_of:]:
+        forward(gi, part, 3)
+    def hole_send(t):
+        q = lax.rem(p + t, Z * K)
+        return remote(hd.at[pl.ds(pl.multiple_of(q * 8, 8), 8), :], hr.at[p], h_send, h_recv, q, w)
+
+    pltpu.make_async_copy(hd.at[pl.ds(pl.multiple_of(p * 8, 8), 8), :], hr.at[p], h_recv).start()
+    loop(1, Z * K, lambda t: hole_send(t).start())
     landed(2)
     both(3)
     landed(3)
     first(lax.rem(z + 4, Z))
 
-    def hole_send(t):
-        q = lax.rem(p + t, Z * K)
-        return remote(hd.at[pl.ds(pl.multiple_of(q * 8, 8), 8), :], hr.at[p], h_send, h_recv, q, w)
-
-    groups = ((0, 3), (3, 5))
 
     def spread(t, e):
         n = lax.rem(chip + t, CHIPS)
-        ds = pl.ds(groups[e][0], groups[e][1] - groups[e][0])
-        return remote(half.at[ds, n], parts.at[chip, ds], r_send, r_recv, z * K + lax.rem(n, 2) * 2 + core, n // 2)
+        ds = pl.ds(SUMS[e][0], SUMS[e][1] - SUMS[e][0])
+        return remote(half.at[ds, n], parts.at[chip, ds], r_send, r_recv.at[e], z * K + lax.rem(n, 2) * 2 + core, n // 2)
 
     def spread_group(e):
-        low, high = groups[e]
+        low, high = SUMS[e]
         for d in range(low, high):
             swap(d).wait_recv()
             half[d] = sums[d, :, core] + sib[d]
         ds = pl.ds(low, high - low)
-        pltpu.make_async_copy(half.at[ds, chip], parts.at[chip, ds], r_recv).start()
+        pltpu.make_async_copy(half.at[ds, chip], parts.at[chip, ds], r_recv.at[e]).start()
         loop(1, CHIPS, lambda t: spread(t, e).start())
 
     def finish(d):
         second(d)
         swap(d).start()
-        pl.when(d == groups[0][1])(lambda: spread_group(0))
+        for e in range(len(SUMS) - 1):
+            pl.when(d == SUMS[e][1])(lambda e=e: spread_group(e))
 
     loop(0, OFFSETS, finish)
-    pltpu.make_async_copy(hd.at[pl.ds(pl.multiple_of(p * 8, 8), 8), :], hr.at[p], h_recv).start()
-    spread_group(1)
-    loop(1, Z * K, lambda t: hole_send(t).start())
-
     wait_bytes(hr, h_recv)
     flat = hr.reshape(Z * K * 8, 4 * cols)
     by_a = [flat[pl.ds(a, Z * K, stride=8), :] for a in range(8)]
@@ -331,47 +336,7 @@
             for e in range(2)]
     for a in range(8):
         hout[pl.ds(a, 64, stride=8), :] = hole[a // 4][:, a % 4 * cols:(a % 4 + 1) * cols]
-
-    wait_bytes(parts, r_recv)
-    total = parts[0]
-    for n in range(1, CHIPS):
-        total = total + parts[n]
-    tall[...] = jnp.zeros_like(tall)
-    for d in range(4):
-        tall[pl.ds(pl.multiple_of(d * 32 + 8 * k, 8), 8), :] = total[d]
-    at[...] = tall[...].T
-    for ww in range(W):
-        for d in range(1, OFFSETS):
-            gb[ww, :, (d - 1) * cols:d * cols] = total[d][:, ww * cols:(ww + 1) * cols]
-
-    def col_send(t):
-        q = lax.rem(p + t, Z * K)
-        return remote(at.at[pl.ds(pl.multiple_of(q * 8, 8), 8), :], slot_a.at[p], f_send, f_recv, q, w)
-
-    def row_send(ww):
-        return remote(gb.at[ww], slot_b.at[z], g_send, g_recv, m, ww)
-
-    def row_here(ww):
-        return jnp.logical_and(m == p, ww == w)
-
-    for ww in range(W):
-        pl.when(row_here(ww))(lambda ww=ww: pltpu.make_async_copy(gb.at[ww], slot_b.at[z], g_recv).start())
-        pl.when(jnp.logical_not(row_here(ww)))(lambda ww=ww: row_send(ww).start())
-    pltpu.make_async_copy(at.at[pl.ds(pl.multiple_of(p * 8, 8), 8), :], slot_a.at[p], f_recv).start()
-    loop(1, Z * K, lambda t: col_send(t).start())
-
-    wait_bytes(slot_b, g_recv)
-    for zz in range(Z):
-        tile = slot_b[zz]
-        for d in range(1, OFFSETS):
-            pair = zz * 8 + (zz + d) % 8
-            out[pair] = tile[:, (d - 1) * cols:d * cols] + hout[pair * 8:pair * 8 + 8, :]
-    wait_bytes(slot_a, f_recv)
-    for zz in range(Z):
-        tile = slot_a[zz * K] + slot_a[zz * K + 1] + slot_a[zz * K + 2] + slot_a[zz * K + 3]
-        for d in range(4):
-            pair = (zz + d) % 8 * 8 + zz
-            out[pair] = tile[:, d * cols:(d + 1) * cols] + hout[pair * 8:pair * 8 + 8, :]
+    spread_group(len(SUMS) - 1)
 
     for gi in range(len(GROUPS)):
         for t in range(1, K):
@@ -391,13 +356,78 @@
     across.wait_send()
     for d in range(OFFSETS):
         swap(d).wait_send()
-    for ww in range(W):
-        pl.when(jnp.logical_not(row_here(ww)))(lambda ww=ww: row_send(ww).wait_send())
     wait_bytes(parts.at[pl.ds(0, CHIPS - 1)], s_send)
     wait_bytes(parts.at[pl.ds(0, CHIPS - 1)], r_send)
     wait_bytes(occs.at[pl.ds(0, W - 1)], q_send)
     wait_bytes(hr.at[pl.ds(0, Z * K - 1)], h_send)
+
+    def gathered(e):
+        low, high = SUMS[e]
+        ds = pl.ds(low, high - low)
+        wait_bytes(parts.at[:, ds], r_recv.at[e])
+        total = parts[0, low:high]
+        for n in range(1, CHIPS):
+            total = total + parts[n, low:high]
+        return [total[n] for n in range(high - low)]
+
+    def col_send(t):
+        q = lax.rem(p + t, Z * K)
+        return remote(at.at[pl.ds(pl.multiple_of(q * 8, 8), 8), :], slot_a.at[p], f_send, f_recv, q, w)
+
+    def row_send(e, ww):
+        src, dst = ((gb, slot_b), (gb4, slot_b4))[e]
+        return remote(src.at[ww], dst.at[z], g_send.at[e], g_recv.at[e], m, ww)
+
+    def row_keep(e, ww):
+        src, dst = ((gb, slot_b), (gb4, slot_b4))[e]
+        return pltpu.make_async_copy(src.at[ww], dst.at[z], g_recv.at[e])
+
+    def rows_start(e):
+        for ww in range(W):
+            here = jnp.logical_and(m == p, ww == w)
+            pl.when(here)(lambda ww=ww: row_keep(e, ww).start())
+            pl.when(jnp.logical_not(here))(lambda ww=ww: row_send(e, ww).start())
+
+    def rows_sent(e):
+        for ww in range(W):
+            here = jnp.logical_and(m == p, ww == w)
+            pl.when(jnp.logical_not(here))(lambda ww=ww: row_send(e, ww).wait_send())
+
+    tall[...] = jnp.zeros_like(tall)
+    total = sum([gathered(e) for e in range(len(SUMS) - 1)], [])
+    for d in range(4):
+        tall[pl.ds(pl.multiple_of(d * 32 + 8 * k, 8), 8), :] = total[d]
+    for ww in range(W):
+        for d in range(1, 4):
+            gb[ww, :, (d - 1) * cols:d * cols] = total[d][:, ww * cols:(ww + 1) * cols]
+    at[...] = tall[...].T
+    pltpu.make_async_copy(at.at[pl.ds(pl.multiple_of(p * 8, 8), 8), :], slot_a.at[p], f_recv).start()
+    loop(1, Z * K, lambda t: col_send(t).start())
+    rows_start(0)
+    last, = gathered(len(SUMS) - 1)
+    for ww in range(W):
+        gb4[ww] = last[:, ww * cols:(ww + 1) * cols]
+    rows_start(1)
+
+    def result(pair, value):
+        out[pair] = value + hout[pair * 8:pair * 8 + 8, :]
+
+    wait_bytes(slot_a, f_recv)
+    for zz in range(Z):
+        tile = slot_a[zz * K] + slot_a[zz * K + 1] + slot_a[zz * K + 2] + slot_a[zz * K + 3]
+        for d in range(4):
+            result((zz + d) % 8 * 8 + zz, tile[:, d * cols:(d + 1) * cols])
+    wait_bytes(slot_b, g_recv.at[0])
+    for zz in range(Z):
+        tile = slot_b[zz]
+        for d in range(1, 4):
+            result(zz * 8 + (zz + d) % 8, tile[:, (d - 1) * cols:d * cols])
     wait_bytes(slot_a.at[pl.ds(0, Z * K - 1)], f_send)
+    rows_sent(0)
+    wait_bytes(slot_b4, g_recv.at[1])
+    for zz in range(Z):
+        result(zz * 8 + (zz + 4) % 8, slot_b4[zz])
+    rows_sent(1)
 
 
 def shards(amplitudes, factors, occ_factors):
@@ -420,14 +450,15 @@
         v((OFFSETS, CHIPS, 8, virt), F32), v((OFFSETS, CHIPS, 8, virt), F32),
         v((CHIPS, OFFSETS, 8, virt), F32),
         v((128, virt), F32), v((virt, 128), F32),
-        v((W, 8, 128), F32), v((Z * K, 8, 128), F32), v((Z, 8, 128), F32),
+        v((W, 8, 3 * cols), F32), v((W, 8, cols), F32),
+        v((Z * K, 8, 128), F32), v((Z, 8, 3 * cols), F32), v((Z, 8, cols), F32),
         v((virt, 128), F32), v((Z * K, 8, 128), F32),
         v((W, occupied * occupied, aux_local), F32),
         v((64, 64), F32), v((64, 64), F32), v((2, 64, 128), F32), v((64 * 8, cols), F32),
         dma(()), dma((len(GROUPS), K)), dma((len(GROUPS), 2)),
         dma(()), dma(()), dma(()), dma(()), dma(()), dma(()),
         dma((2, len(GROUPS), 2)), dma((2, len(GROUPS), 2, 4)), dma((2, len(GROUPS), 2, 4)),
-        dma(()), dma(()), dma(()), dma(()), dma((OFFSETS,)), dma((OFFSETS,)), dma(()), dma(()), dma(()), dma(()), dma(()), dma(()),
+        dma(()), dma(()), dma(()), dma(()), dma((OFFSETS,)), dma((OFFSETS,)), dma(()), dma((len(SUMS),)), dma(()), dma(()), dma((2,)), dma((2,)),
     ]
     return pl.pallas_call(
         kernel,
@@ -436,9 +467,9 @@
         out_specs=vm,
         scratch_shapes=scratch,
         compiler_params=pltpu.CompilerParams(
-            collective_id=0, has_side_effects=True, vmem_limit_bytes=(64 << 20) - (330 << 10)),
+            collective_id=0, has_side_effects=True, vmem_limit_bytes=48 << 20),
         name="residual",
-    )(amplitudes, factors, occ)
+    )(pltpu.with_memory_space_constraint(amplitudes, pltpu.HBM), pltpu.with_memory_space_constraint(factors, pltpu.HBM), occ)
 
 
 def solution(mesh):

time: 82.2 us -> 78.2 us (0.951)
  Pallas kernels: 80.3 us -> 76.3 us
    pallas_call x1, Pallas kernels: 80.3 us -> 76.3 us  [shards(): pl.pallas_call(kernel, out_shape=jax.ShapeDtypeStruct((occupied * occupie...]
    pallas_call x1, local copies, waits for them, and re-layouts: 1.73 us -> 0.8 us  [shards(): pl.pallas_call(kernel, out_shape=jax.ShapeDtypeStruct((occupied * occupie...]
where the time goes in v4:
time: 78.2 us; the launch traced here: 77.9 us
  Pallas kernels  76.3 us (98%)
  local copies, waits for them, and re-layouts  1.56 us (2%)
    pallas_call x1, Pallas kernels, shards(): pl.pallas_call(kernel, out_shape=jax.ShapeDtypeStruct((occupied * occupie...  76.3 us

profile of v4, /device:TPU:1, one launch (start us, length us, event | category | flops | bytes accessed | tf_op | source)
XLA Modules:
  0.0 77.9 jit_solution(18301004030648736835)
XLA Ops:
  0.0 0.0 copy-start
  0.0 0.8 copy-done
  0.8 76.3 %residual.1 = f32[64,8,32]{2,1,0:T(8,128)S(1)} custom-call(f32[2,256,256]{2,1,0:T(8,128)} %amp_hbm.1, f32[48,8,256]{2,1,0:T(8,128)} %fac.1, f32[64,48]{1,0:T(8,128)S(1)} %bitcast.3), custom_call_target="tpu_custom_call" | custom-call | tf_op jit(solution)/shard_map/residual/pallas_call | solution.py:463
  77.1 0.8 %copy.4 = f32[64,8,32]{0,2,1:T(8,128)} copy(f32[64,8,32]{2,1,0:T(8,128)S(1)} %residual.1) | data formatting | bytes 131072 | tf_op jit(solution)/shard_map/residual/pallas_call | solution.py:463
Async XLA Ops:
  0.0 0.8 copy-start

commit v5 on v4

--- a/solution.py
+++ b/solution.py
@@ -81,7 +81,7 @@
 
 def kernel(amp_hbm, fac, occ, out,
            amp, flip, slots, mine, sall, ball, s3, b3, y3, acc,
-           sib, half, parts, tall, at, gb, gb4, slot_a, slot_b, slot_b4, hd, hr, occs, gm, cm, hs, hout,
+           sib, half, parts, at, gb, gb4, slot_a, slot_b, slot_b4, hd, hr, occs, gm, cm, hs, hout,
            in_sem, ex_send, ex_recv, a_send, a_recv, s_send, s_recv, w_send, w_recv, l_send, ring_send, ring_recv,
            q_send, q_recv, h_send, h_recv, c_send, c_recv, r_send, r_recv, f_send, f_recv, g_send, g_recv):
     p = lax.axis_index("pairs")
@@ -289,11 +289,29 @@
         q = lax.rem(p + t, Z * K)
         return remote(hd.at[pl.ds(pl.multiple_of(q * 8, 8), 8), :], hr.at[p], h_send, h_recv, q, w)
 
-    pltpu.make_async_copy(hd.at[pl.ds(pl.multiple_of(p * 8, 8), 8), :], hr.at[p], h_recv).start()
-    loop(1, Z * K, lambda t: hole_send(t).start())
+    for gi in range(len(GROUPS)):
+        for t in range(1, K):
+            exchange(gi, t).wait_send()
+        for way in range(2):
+            for t in range(2):
+                launch(way, gi, t).wait_send()
+            for part in range(2):
+                for h in range(1 - part, 3):
+                    ring(way, gi, part, h).wait_send()
+    for t in range(1, K):
+        straight(t).wait_send()
+    for s in range(2):
+        for kk in range(K):
+            here = jnp.logical_and(2 * k + s == z, kk == k)
+            pl.when(jnp.logical_not(here))(lambda s=s, kk=kk: turned_far(s, kk).wait_send())
+    across.wait_send()
+    wait_bytes(parts.at[pl.ds(0, CHIPS - 1)], s_send)
+    wait_bytes(occs.at[pl.ds(0, W - 1)], q_send)
     landed(2)
     both(3)
     landed(3)
+    pltpu.make_async_copy(hd.at[pl.ds(pl.multiple_of(p * 8, 8), 8), :], hr.at[p], h_recv).start()
+    loop(1, Z * K, lambda t: hole_send(t).start())
     first(lax.rem(z + 4, Z))
 
 
@@ -336,30 +354,17 @@
             for e in range(2)]
     for a in range(8):
         hout[pl.ds(a, 64, stride=8), :] = hole[a // 4][:, a % 4 * cols:(a % 4 + 1) * cols]
+
     spread_group(len(SUMS) - 1)
 
     for gi in range(len(GROUPS)):
-        for t in range(1, K):
-            exchange(gi, t).wait_send()
         for way in range(2):
-            for t in range(2):
-                launch(way, gi, t).wait_send()
             for part in range(2):
-                for h in range(1 - part, hops(way, gi, part)):
-                    ring(way, gi, part, h).wait_send()
-    for t in range(1, K):
-        straight(t).wait_send()
-    for s in range(2):
-        for kk in range(K):
-            here = jnp.logical_and(2 * k + s == z, kk == k)
-            pl.when(jnp.logical_not(here))(lambda s=s, kk=kk: turned_far(s, kk).wait_send())
-    across.wait_send()
+                if hops(way, gi, part) == 4:
+                    ring(way, gi, part, 3).wait_send()
     for d in range(OFFSETS):
         swap(d).wait_send()
-    wait_bytes(parts.at[pl.ds(0, CHIPS - 1)], s_send)
     wait_bytes(parts.at[pl.ds(0, CHIPS - 1)], r_send)
-    wait_bytes(occs.at[pl.ds(0, W - 1)], q_send)
-    wait_bytes(hr.at[pl.ds(0, Z * K - 1)], h_send)
 
     def gathered(e):
         low, high = SUMS[e]
@@ -393,14 +398,11 @@
             here = jnp.logical_and(m == p, ww == w)
             pl.when(jnp.logical_not(here))(lambda ww=ww: row_send(e, ww).wait_send())
 
-    tall[...] = jnp.zeros_like(tall)
     total = sum([gathered(e) for e in range(len(SUMS) - 1)], [])
-    for d in range(4):
-        tall[pl.ds(pl.multiple_of(d * 32 + 8 * k, 8), 8), :] = total[d]
     for ww in range(W):
         for d in range(1, 4):
             gb[ww, :, (d - 1) * cols:d * cols] = total[d][:, ww * cols:(ww + 1) * cols]
-    at[...] = tall[...].T
+    at[...] = jnp.concatenate(total[:4], axis=0).T
     pltpu.make_async_copy(at.at[pl.ds(pl.multiple_of(p * 8, 8), 8), :], slot_a.at[p], f_recv).start()
     loop(1, Z * K, lambda t: col_send(t).start())
     rows_start(0)
@@ -414,9 +416,9 @@
 
     wait_bytes(slot_a, f_recv)
     for zz in range(Z):
-        tile = slot_a[zz * K] + slot_a[zz * K + 1] + slot_a[zz * K + 2] + slot_a[zz * K + 3]
+        tiles = [slot_a[zz * K + kk] for kk in range(K)]
         for d in range(4):
-            result((zz + d) % 8 * 8 + zz, tile[:, d * cols:(d + 1) * cols])
+            result((zz + d) % 8 * 8 + zz, jnp.concatenate([tile[:, d * 8:d * 8 + 8] for tile in tiles], axis=1))
     wait_bytes(slot_b, g_recv.at[0])
     for zz in range(Z):
         tile = slot_b[zz]
@@ -428,6 +430,7 @@
     for zz in range(Z):
         result(zz * 8 + (zz + 4) % 8, slot_b4[zz])
     rows_sent(1)
+    wait_bytes(hr.at[pl.ds(0, Z * K - 1)], h_send)
 
 
 def shards(amplitudes, factors, occ_factors):
@@ -449,9 +452,9 @@
         v((OFFSETS * virt, virt), F32),
         v((OFFSETS, CHIPS, 8, virt), F32), v((OFFSETS, CHIPS, 8, virt), F32),
         v((CHIPS, OFFSETS, 8, virt), F32),
-        v((128, virt), F32), v((virt, 128), F32),
+        v((virt, 32), F32),
         v((W, 8, 3 * cols), F32), v((W, 8, cols), F32),
-        v((Z * K, 8, 128), F32), v((Z, 8, 3 * cols), F32), v((Z, 8, cols), F32),
+        v((Z * K, 8, 32), F32), v((Z, 8, 3 * cols), F32), v((Z, 8, cols), F32),
         v((virt, 128), F32), v((Z * K, 8, 128), F32),
         v((W, occupied * occupied, aux_local), F32),
         v((64, 64), F32), v((64, 64), F32), v((2, 64, 128), F32), v((64 * 8, cols), F32),
@@ -463,13 +466,14 @@
     return pl.pallas_call(
         kernel,
         out_shape=jax.ShapeDtypeStruct((occupied * occupied, rows, cols), F32),
-        in_specs=[anywhere, anywhere, vm],
+        in_specs=[anywhere, anywhere, anywhere],
         out_specs=vm,
         scratch_shapes=scratch,
         compiler_params=pltpu.CompilerParams(
             collective_id=0, has_side_effects=True, vmem_limit_bytes=48 << 20),
         name="residual",
-    )(pltpu.with_memory_space_constraint(amplitudes, pltpu.HBM), pltpu.with_memory_space_constraint(factors, pltpu.HBM), occ)
+    )(pltpu.with_memory_space_constraint(amplitudes, pltpu.HBM), pltpu.with_memory_space_constraint(factors, pltpu.HBM),
+      pltpu.with_memory_space_constraint(occ, pltpu.HBM))
 
 
 def solution(mesh):

time: 78.2 us -> 77.2 us (0.987)
  no operation moved by 1% of the time
where the time goes in v5:
time: 77.2 us; the launch traced here: 76.9 us
  Pallas kernels  76.1 us (99%)
  local copies, waits for them, and re-layouts  0.8 us (1%)
    pallas_call x1, Pallas kernels, shards(): pl.pallas_call(kernel, out_shape=jax.ShapeDtypeStruct((occupied * occupie...  76.1 us

profile of v5, /device:TPU:1, one launch (start us, length us, event | category | flops | bytes accessed | tf_op | source)
XLA Modules:
  0.0 76.9 jit_solution(1378479066610611007)
XLA Ops:
  0.0 76.1 %residual.1 = f32[64,8,32]{2,1,0:T(8,128)S(1)} custom-call(f32[2,256,256]{2,1,0:T(8,128)} %amp_hbm.1, f32[48,8,256]{2,1,0:T(8,128)} %fac.1, f32[64,48]{1,0:T(8,128)} %bitcast.3), custom_call_target="tpu_custom_call" | custom-call | tf_op jit(solution)/shard_map/residual/pallas_call | solution.py:466
  76.1 0.8 %copy.4 = f32[64,8,32]{0,2,1:T(8,128)} copy(f32[64,8,32]{2,1,0:T(8,128)S(1)} %residual.1) | data formatting | bytes 131072 | tf_op jit(solution)/shard_map/residual/pallas_call | solution.py:466

commit v6 on v5

--- a/solution.py
+++ b/solution.py
@@ -50,8 +50,8 @@
             barrier, inc=1, device_id={"pairs": lax.rem(p + t, Z * K), "aux": w},
             device_id_type=pl.DeviceIdType.MESH)
 
-    loop(1, CHIPS, plane_peer)
-    loop(1, Z * K, column_peer)
+    many(1, CHIPS, plane_peer)
+    many(1, Z * K, column_peer)
 
 
 def met():
@@ -64,6 +64,19 @@
         return c
 
     lax.fori_loop(start, stop, step, 0)
+
+
+def many(start, stop, body, wide=5):
+    whole = (stop - start) // wide
+
+    def step(n, c):
+        for u in range(wide):
+            body(start + n * wide + u)
+        return c
+
+    lax.fori_loop(0, whole, step, 0)
+    for t in range(start + whole * wide, stop):
+        body(t)
 
 
 def split(x):
@@ -206,7 +219,7 @@
         j = lax.rem(z + d, Z)
         mine[d] = slots[j] + slots[Z + j]
     pltpu.make_async_copy(mine, sall.at[:, chip, core], s_recv).start()
-    loop(1, CHIPS, lambda t: share(t).start())
+    many(1, CHIPS, lambda t: share(t).start())
     for part in range(2):
         for gi in range(len(GROUPS)):
             forward(gi, part, 1)
@@ -215,7 +228,7 @@
         return remote(occ, occs.at[w], q_send, q_recv, p, lax.rem(w + t, W))
 
     pltpu.make_async_copy(occ, occs.at[w], q_recv).start()
-    loop(1, W, lambda t: occ_share(t).start())
+    many(1, W, lambda t: occ_share(t).start())
     at_w = pl.ds(pl.multiple_of(w * cols, cols), cols)
     for s in range(2):
         hd[:, s * cols:(s + 1) * cols] = flip[s, at_w, :].T
@@ -311,7 +324,7 @@
     both(3)
     landed(3)
     pltpu.make_async_copy(hd.at[pl.ds(pl.multiple_of(p * 8, 8), 8), :], hr.at[p], h_recv).start()
-    loop(1, Z * K, lambda t: hole_send(t).start())
+    many(1, Z * K, lambda t: hole_send(t).start())
     first(lax.rem(z + 4, Z))
 
 
@@ -327,7 +340,7 @@
             half[d] = sums[d, :, core] + sib[d]
         ds = pl.ds(low, high - low)
         pltpu.make_async_copy(half.at[ds, chip], parts.at[chip, ds], r_recv.at[e]).start()
-        loop(1, CHIPS, lambda t: spread(t, e).start())
+        many(1, CHIPS, lambda t: spread(t, e).start())
 
     def finish(d):
         second(d)
@@ -404,7 +417,7 @@
             gb[ww, :, (d - 1) * cols:d * cols] = total[d][:, ww * cols:(ww + 1) * cols]
     at[...] = jnp.concatenate(total[:4], axis=0).T
     pltpu.make_async_copy(at.at[pl.ds(pl.multiple_of(p * 8, 8), 8), :], slot_a.at[p], f_recv).start()
-    loop(1, Z * K, lambda t: col_send(t).start())
+    many(1, Z * K, lambda t: col_send(t).start())
     rows_start(0)
     last, = gathered(len(SUMS) - 1)
     for ww in range(W):

time: 77.2 us -> 76.7 us (level)
  no operation moved by 1% of the time
where the time goes in v6:
time: 76.7 us; the launch traced here: 76.2 us
  Pallas kernels  75.4 us (98%)
  local copies, waits for them, and re-layouts  0.8 us (1%)
    pallas_call x1, Pallas kernels, shards(): pl.pallas_call(kernel, out_shape=jax.ShapeDtypeStruct((occupied * occupie...  75.4 us

profile of v6, /device:TPU:1, one launch (start us, length us, event | category | flops | bytes accessed | tf_op | source)
XLA Modules:
  0.0 76.2 jit_solution(645633776144539964)
XLA Ops:
  0.0 75.4 %residual.1 = f32[64,8,32]{2,1,0:T(8,128)S(1)} custom-call(f32[2,256,256]{2,1,0:T(8,128)} %amp_hbm.1, f32[48,8,256]{2,1,0:T(8,128)} %fac.1, f32[64,48]{1,0:T(8,128)} %bitcast.3), custom_call_target="tpu_custom_call" | custom-call | tf_op jit(solution)/shard_map/residual/pallas_call | solution.py:479
  75.4 0.8 %copy.4 = f32[64,8,32]{0,2,1:T(8,128)} copy(f32[64,8,32]{2,1,0:T(8,128)S(1)} %residual.1) | data formatting | bytes 131072 | tf_op jit(solution)/shard_map/residual/pallas_call | solution.py:479

commit v7 on v6

--- a/solution.py
+++ b/solution.py
@@ -268,7 +268,8 @@
                 y3[d, rows, at_q + virt:at_q + 2 * virt] = y_lo[q * 32:(q + 1) * 32]
                 y3[d, rows, at_q + 2 * virt:at_q + 3 * virt] = y_hi[q * 32:(q + 1) * 32]
 
-        loop(0, OFFSETS, one)
+        for d in range(OFFSETS):
+            one(d)
 
     def both(step):
         loop(0, 2, lambda t: first(lax.rem(z + step + t * (Z - 2 * step), Z)))

time: 76.7 us -> 72.7 us (0.948)
  Pallas kernels: 75.4 us -> 71 us
    pallas_call x1, Pallas kernels: 75.4 us -> 71 us  [shards(): pl.pallas_call(kernel, out_shape=jax.ShapeDtypeStruct((occupied * occupie...]
where the time goes in v7:
time: 72.7 us; the launch traced here: 71.8 us
  Pallas kernels  71 us (98%)
  local copies, waits for them, and re-layouts  0.8 us (1%)
    pallas_call x1, Pallas kernels, shards(): pl.pallas_call(kernel, out_shape=jax.ShapeDtypeStruct((occupied * occupie...  71 us

profile of v7, /device:TPU:1, one launch (start us, length us, event | category | flops | bytes accessed | tf_op | source)
XLA Modules:
  0.0 71.8 jit_solution(587784547788633898)
XLA Ops:
  0.0 71.0 %residual.1 = f32[64,8,32]{2,1,0:T(8,128)S(1)} custom-call(f32[2,256,256]{2,1,0:T(8,128)} %amp_hbm.1, f32[48,8,256]{2,1,0:T(8,128)} %fac.1, f32[64,48]{1,0:T(8,128)} %bitcast.3), custom_call_target="tpu_custom_call" | custom-call | tf_op jit(solution)/shard_map/residual/pallas_call | solution.py:480
  71.0 0.8 %copy.4 = f32[64,8,32]{0,2,1:T(8,128)} copy(f32[64,8,32]{2,1,0:T(8,128)S(1)} %residual.1) | data formatting | bytes 131072 | tf_op jit(solution)/shard_map/residual/pallas_call | solution.py:480
